TPU v7x, 32 devices: a whole 2x2x4 slice. The times are simulated.
32 devices in a mesh: harm: 16 (over z, x, core), bus: 2 (over y).
Axes of the slice: x: 2, y: 2, z: 4, core: 2. Of those that a mesh axis runs over, the one named last changes fastest.
Arguments:
- conv_volt: bfloat16 [2, 64, 128, 128], P(None, None, ('bus', 'harm')), may hold values from -0.75 to 0.75
- conv_power: float32 [128, 128], P(('bus', 'harm')), may hold values from 0.2 to 2
- conv_type: int32 [128], P(('bus', 'harm')), may hold values from 0 to 7
- type_steep: float32 [8], replicated, may hold values from 0.5 to 4
- conv_bus: int32 [128], P(('bus', 'harm')), may hold values from 0 to 511, as said below
- admittance: float32 [2, 4, 64, 512], P(None, None, 'harm', 'bus'), may hold values from -0.5 to 1
- link_offset: int32 [3, 512], P(None, 'bus'), may hold values from -8 to 8, as said below
Outputs:
- bus_volt: bfloat16 [2, 64, 512, 128], P(None, 'harm', 'bus')
- conv_next: bfloat16 [2, 64, 128, 128], P(None, None, ('bus', 'harm'))
Inputs may be any that keep to these rules, and one draw needn't show every extreme that they name: `conv_bus`: converter c is attached to one of the buses from (c // 4) * 16 to (c // 4 + 1) * 16 - 1; a bus may carry several converters. `link_offset`: the first line of every bus spans exactly 8 buses, up or down; the others span 1 to 8 buses; no offset is zero.
All inputs are finite; a program needn't handle non-finite values.
Results may differ from a plain program's by a relative error of at most 0.0057.
Values may be sent and summed in bfloat16 or wider, within the bound.
A program may use at most 64 MiB of HBM per device.

v0:
```python
import functools
import math

import jax
import jax.numpy as jnp
import numpy as np
from jax import lax
from jax.experimental import pallas as pl
from jax.experimental.pallas import tpu as pltpu
from jax.sharding import PartitionSpec as P

NT = 1024
LANES = 128
CHUNKS = 4


def make_basis(orders):
    samples = np.arange(NT)
    phases = (np.arange(1, orders + 1)[:, None] * samples[None, :] % NT) * (2.0 * math.pi / NT)
    return np.concatenate([np.cos(phases), -np.sin(phases)], axis=0).astype(np.float32)


def kernel(
    nh,
    ny,
    volt_ref,
    power_ref,
    type_ref,
    steep_ref,
    bus_ref,
    adm_ref,
    off_ref,
    fwd_ref,
    inv_ref,
    perm_ref,
    back_ref,
    out_ref,
    next_ref,
    volts,
    send,
    recv,
    my_bus,
    buses,
    adm_side,
    off_side,
    weights,
    resp,
    send_back,
    spec_send,
    spec_recv,
    left_send,
    right_send,
    bus_send,
    bus_recv,
    bus_left,
    bus_right,
    side_send,
    side_recv,
    ret_send,
    ret_recv,
    local_sem,
):
    me = lax.axis_index("harm")
    y = lax.axis_index("bus")
    hl = adm_ref.shape[2]
    block = adm_ref.shape[3]
    links = off_ref.shape[0]
    conv = power_ref.shape[0]
    sub = block // nh
    tiles = block // LANES
    around = LANES // sub
    rows = 8 * (around + 2)
    has_left = y > 0
    has_right = y < ny - 1

    barrier = pltpu.get_barrier_semaphore()

    def greet(d, by):
        pl.semaphore_signal(barrier, inc=1, device_id={"harm": d, "bus": by})

    def greet_peer(s, carry):
        greet(lax.rem(me + s, nh), y)
        return carry

    lax.fori_loop(1, nh, greet_peer, 0)

    @pl.when(has_left)
    def _():
        lax.fori_loop(0, nh, lambda d, c: (greet(d, y - 1), c)[1], 0)

    @pl.when(has_right)
    def _():
        lax.fori_loop(0, nh, lambda d, c: (greet(d, y + 1), c)[1], 0)

    first = (y * nh + me) * sub
    row8 = lax.broadcasted_iota(jnp.int32, (8, LANES), 0) % conv
    numbers = jnp.zeros((8, LANES), jnp.float32)
    for c in range(conv):
        numbers = jnp.where(row8 == c, (bus_ref[c] - first).astype(jnp.float32), numbers)
    my_bus[...] = numbers.astype(jnp.bfloat16)

    @pl.when(jnp.logical_not(has_left))
    def _():
        recv[0] = jnp.zeros(recv.shape[1:], recv.dtype)
        buses[0] = jnp.zeros(buses.shape[1:], buses.dtype)
        adm_side[0] = jnp.zeros(adm_side.shape[1:], adm_side.dtype)
        off_side[0] = jnp.zeros(off_side.shape[1:], off_side.dtype)

    @pl.when(jnp.logical_not(has_right))
    def _():
        recv[nh + 1] = jnp.zeros(recv.shape[1:], recv.dtype)
        buses[nh + 1] = jnp.zeros(buses.shape[1:], buses.dtype)
        adm_side[1] = jnp.zeros(adm_side.shape[1:], adm_side.dtype)
        off_side[1] = jnp.zeros(off_side.shape[1:], off_side.dtype)

    lane = lax.broadcasted_iota(jnp.int32, (1, LANES), 1)
    is_right = lane < LANES // 2

    def adm_row(p, k, h, t, beyond):
        def row_of(t):
            if t < 0:
                return adm_side[0, p, k, h : h + 1, :]
            if t >= tiles:
                return adm_side[1, p, k, h : h + 1, :]
            return adm_ref[p, k, h : h + 1, LANES * t : LANES * (t + 1)]

        return jnp.where(is_right, row_of(t + 1), row_of(t - 1)) if beyond else row_of(t)

    def off_row(k, t, beyond):
        def row_of(t):
            if t < 0:
                return off_side[0, k : k + 1, :]
            if t >= tiles:
                return off_side[1, k : k + 1, :]
            return off_ref[k : k + 1, LANES * t : LANES * (t + 1)]

        return jnp.where(is_right, row_of(t + 1), row_of(t - 1)) if beyond else row_of(t)

    def fill(t, beyond, low, high):
        band = lax.broadcasted_iota(jnp.int32, (high - low, LANES), 0) + low
        shift = LANES if beyond else 0
        masks = [
            band == jnp.bitwise_and(lane + shift + off_row(k, t, beyond), 2 * LANES - 1) for k in range(links)
        ]
        at = 2 * shift
        for h in range(hl):
            d_real, d_imag = adm_row(0, 0, h, t, beyond), adm_row(1, 0, h, t, beyond)
            total_real = jnp.zeros(band.shape, jnp.float32)
            total_imag = jnp.zeros(band.shape, jnp.float32)
            for k in range(links):
                l_real, l_imag = adm_row(0, 1 + k, h, t, beyond), adm_row(1, 1 + k, h, t, beyond)
                total_real += jnp.where(masks[k], d_real * l_real - d_imag * l_imag, 0.0)
                total_imag += jnp.where(masks[k], d_real * l_imag + d_imag * l_real, 0.0)
            weights[h, t, low:high, at : at + LANES] = total_real.astype(jnp.bfloat16)
            weights[h, t, low:high, at + LANES : at + 2 * LANES] = total_imag.astype(jnp.bfloat16)

    for t in range(tiles):
        fill(t, False, 0, LANES + 16)
        fill(t, False, 2 * LANES - 16, 2 * LANES)
        for h in range(hl):
            weights[h, t, LANES + 16 : 2 * LANES - 16, :] = jnp.zeros((LANES - 32, 4 * LANES), jnp.bfloat16)
            weights[h, t, 16 : LANES - 16, 2 * LANES :] = jnp.zeros((LANES - 32, 2 * LANES), jnp.bfloat16)

    pl.semaphore_wait(barrier, nh - 1 + nh * has_left.astype(jnp.int32) + nh * has_right.astype(jnp.int32))

    def remote(src, dst, send_sem, recv_sem, d, by):
        return pltpu.make_async_remote_copy(
            src_ref=src, dst_ref=dst, send_sem=send_sem, recv_sem=recv_sem, device_id={"harm": d, "bus": by}
        )

    def bus_copy(d, slot, by, sems):
        return remote(my_bus, buses.at[slot], sems.at[d], bus_recv.at[slot], d, by)

    def spec_copy(d, slot, by, sems):
        return remote(send.at[d], recv.at[slot], sems.at[d], spec_recv.at[slot], d, by)

    def ret_copy(d, source):
        place = next_ref.at[:, pl.ds(source * hl, hl)]
        return remote(send_back.at[d], place, ret_send.at[d], ret_recv.at[source], d, y)

    def side_copies(side):
        by = y + 1 if side == 0 else y - 1
        start = block - LANES if side == 0 else 0
        return (
            remote(
                adm_ref.at[:, :, :, pl.ds(start, LANES)],
                adm_side.at[side],
                side_send.at[side],
                side_recv.at[side],
                me,
                by,
            ),
            remote(
                off_ref.at[:, pl.ds(start, LANES)],
                off_side.at[side],
                side_send.at[2 + side],
                side_recv.at[2 + side],
                me,
                by,
            ),
        )

    send_right = jnp.logical_and(has_right, me == nh - 1)
    send_left = jnp.logical_and(has_left, me == 0)

    def each(low, body):
        def step(i, carry):
            body(i)
            return carry

        lax.fori_loop(low, nh, step, 0)

    def peer(s):
        return lax.rem(me + s, nh)

    each(1, lambda s: bus_copy(peer(s), me + 1, y, bus_send).start())

    @pl.when(send_right)
    def _():
        each(0, lambda d: bus_copy(d, 0, y + 1, bus_right).start())

    @pl.when(send_left)
    def _():
        each(0, lambda d: bus_copy(d, nh + 1, y - 1, bus_left).start())

    @pl.when(has_right)
    def _():
        for copy in side_copies(0):
            copy.start()

    @pl.when(has_left)
    def _():
        for copy in side_copies(1):
            copy.start()

    span = volt_ref.shape[0] // conv
    per = LANES // conv
    for b in range(span // per):
        block_rows = jnp.dot(
            perm_ref[...], volt_ref[LANES * b : LANES * (b + 1), :], preferred_element_type=jnp.float32
        ).astype(jnp.bfloat16)
        for c in range(conv):
            volts[per * b : per * (b + 1), LANES * c : LANES * (c + 1)] = block_rows[per * c : per * (c + 1), :]
    steep = jnp.concatenate(
        [jnp.full((1, LANES), steep_ref[type_ref[c]], jnp.float32) for c in range(conv)], axis=1
    )
    power = jnp.concatenate([power_ref[c : c + 1, :] for c in range(conv)], axis=1) * NT ** (-0.5)
    part = NT // CHUNKS
    spectra = jnp.zeros((span, conv * LANES), jnp.float32)
    for q in range(CHUNKS):
        wave = jnp.dot(fwd_ref[part * q : part * (q + 1), :], volts[...], preferred_element_type=jnp.float32)
        now = jnp.tanh(steep * wave).astype(jnp.bfloat16)
        spectra = spectra + jnp.dot(
            inv_ref[:, part * q : part * (q + 1)], now, preferred_element_type=jnp.float32
        )
    spectra = (spectra * power).astype(jnp.bfloat16)
    per_dev = 8 * hl
    for b in range(span // per):
        stacked = jnp.concatenate(
            [spectra[per * b : per * (b + 1), LANES * c : LANES * (c + 1)] for c in range(conv)], axis=0
        )
        mixed = jnp.dot(back_ref[...], stacked, preferred_element_type=jnp.float32)
        count = LANES // per_dev
        send[count * b : count * (b + 1)] = mixed.reshape(count, hl, 8, LANES).astype(jnp.bfloat16)

    each(1, lambda s: spec_copy(peer(s), me + 1, y, spec_send).start())

    @pl.when(send_right)
    def _():
        each(0, lambda d: spec_copy(d, 0, y + 1, left_send).start())

    @pl.when(send_left)
    def _():
        each(0, lambda d: spec_copy(d, nh + 1, y - 1, right_send).start())

    recv[me + 1] = send[me]
    buses[me + 1] = my_bus[...]

    @pl.when(has_left)
    def _():
        for copy in side_copies(0):
            copy.wait_recv()

    @pl.when(has_right)
    def _():
        for copy in side_copies(1):
            copy.wait_recv()

    for t in range(tiles):
        for low, high in ((LANES - 16, LANES + 16), (2 * LANES - 16, 2 * LANES), (0, 16)):
            fill(t, True, low, high)

    each(1, lambda s: bus_copy(peer(s), peer(s) + 1, y, bus_send).wait_recv())

    @pl.when(has_left)
    def _():
        bus_copy(0, 0, y, bus_send).wait_recv()

    @pl.when(has_right)
    def _():
        bus_copy(0, nh + 1, y, bus_send).wait_recv()

    row = lax.broadcasted_iota(jnp.int32, (rows, LANES), 0)
    is_real = row % 8 < conv
    base = jnp.bitwise_and((row // 8 - 1) * sub, 2 * LANES - 1)
    own = 8 * around
    for t in range(tiles):
        near = buses[around * t : around * (t + 1) + 2].astype(jnp.float32).reshape(rows, LANES)
        at_bus = base + near.astype(jnp.int32)
        hits = [at_bus == lane, at_bus == lane + LANES]
        picked = jnp.where(hits[0], 1.0, 0.0)
        pick_real = jnp.where(is_real, picked, 0.0)[8 : 8 + own].astype(jnp.bfloat16)
        pick_imag = jnp.where(is_real, 0.0, picked)[8 : 8 + own].astype(jnp.bfloat16)
        for h in range(hl):
            start_real, start_imag = [], []
            for side in (False, True):
                d_real, d_imag = adm_row(0, 0, h, t, side), adm_row(1, 0, h, t, side)
                start_real.append(jnp.where(hits[side], jnp.where(is_real, d_real, -d_imag), 0.0))
                start_imag.append(jnp.where(hits[side], jnp.where(is_real, d_imag, d_real), 0.0))
            now_real, now_imag = start_real, start_imag
            for last in (False, True):
                state = jnp.concatenate(
                    [jnp.concatenate(now_real, axis=1), jnp.concatenate(now_imag, axis=1)], axis=0
                ).astype(jnp.bfloat16)
                width = 2 * LANES if last else 4 * LANES
                both = jnp.dot(state, weights[h, t, :, 0:width], preferred_element_type=jnp.float32)
                new_real, new_imag = [], []
                for a in range(1 if last else 2):
                    at = 2 * LANES * a
                    left, right = both[:, at : at + LANES], both[:, at + LANES : at + 2 * LANES]
                    new_real.append(start_real[a] + left[:rows] - right[rows:])
                    new_imag.append(start_imag[a] + right[:rows] + left[rows:])
                now_real, now_imag = new_real, new_imag
            real_t = now_real[0].T.astype(jnp.bfloat16)
            imag_t = now_imag[0].T.astype(jnp.bfloat16)
            resp[h, t, own : own + LANES, :] = real_t
            resp[h, t, own + LANES :, :] = imag_t
            chosen = jnp.dot(pick_real, real_t, preferred_element_type=jnp.float32)
            chosen += jnp.dot(pick_imag, imag_t, preferred_element_type=jnp.float32)
            resp[h, t, 0:own, :] = chosen.astype(jnp.bfloat16)

    each(1, lambda s: spec_copy(peer(s), peer(s) + 1, y, spec_send).wait_recv())

    @pl.when(has_left)
    def _():
        spec_copy(0, 0, y, spec_send).wait_recv()

    @pl.when(has_right)
    def _():
        spec_copy(0, nh + 1, y, spec_send).wait_recv()

    arrived = []
    for t in range(tiles):
        for h in range(hl):
            here = recv[around * t : around * (t + 1) + 2, h].astype(jnp.float32)
            arrived.append(here.reshape(rows, LANES).astype(jnp.bfloat16))
            at_conv = jnp.dot(resp[h, t, 0:own, :], arrived[-1], preferred_element_type=jnp.float32)
            at_conv = at_conv.reshape(around, 2, conv, LANES).astype(jnp.bfloat16)
            send_back[around * t : around * (t + 1), :, h] = at_conv
    each(1, lambda s: ret_copy(peer(s), me).start())
    keep = pltpu.make_async_copy(send_back.at[me], next_ref.at[:, pl.ds(me * hl, hl)], local_sem)
    keep.start()
    for t in range(tiles):
        for h in range(hl):
            solved = jnp.dot(resp[h, t, own:, :], arrived[t * hl + h], preferred_element_type=jnp.float32)
            out_ref[:, h, LANES * t : LANES * (t + 1)] = solved.astype(jnp.bfloat16).reshape(2, LANES, LANES)

    each(1, lambda s: bus_copy(peer(s), me + 1, y, bus_send).wait_send())
    each(1, lambda s: spec_copy(peer(s), me + 1, y, spec_send).wait_send())

    @pl.when(has_right)
    def _():
        for copy in side_copies(0):
            copy.wait_send()

    @pl.when(has_left)
    def _():
        for copy in side_copies(1):
            copy.wait_send()

    @pl.when(send_right)
    def _():
        each(0, lambda d: bus_copy(d, 0, y + 1, bus_right).wait_send())
        each(0, lambda d: spec_copy(d, 0, y + 1, left_send).wait_send())

    @pl.when(send_left)
    def _():
        each(0, lambda d: bus_copy(d, nh + 1, y - 1, bus_left).wait_send())
        each(0, lambda d: spec_copy(d, nh + 1, y - 1, right_send).wait_send())

    keep.wait()
    each(1, lambda s: ret_copy(peer(s), me).wait_send())
    each(1, lambda s: ret_copy(peer(s), peer(s)).wait_recv())


def store(volt_ref, next_ref, volt_out, next_out, sems):
    copies = [pltpu.make_async_copy(volt_ref.at[p], volt_out.at[p], sems.at[p]) for p in range(2)]
    copies.append(pltpu.make_async_copy(next_ref, next_out, sems.at[2]))
    for copy in copies:
        copy.start()
    for copy in copies:
        copy.wait()


def local(nh, ny, conv_volt, conv_power, conv_type, type_steep, conv_bus, admittance, link_offset):
    _, orders, conv, snaps = conv_volt.shape
    hl = orders // nh
    block = admittance.shape[3]
    tiles = block // LANES
    around = LANES * nh // block
    rows = 8 * (around + 2)
    span = 2 * orders
    basis = make_basis(orders)
    regrouped = basis.reshape(2, orders, NT).transpose(1, 0, 2).reshape(span, NT)
    per = LANES // conv
    perm = np.zeros((LANES, LANES), np.float32)
    for c in range(conv):
        for k in range(per):
            perm[per * c + k, conv * k + c] = 1.0
    vmem = pl.BlockSpec(memory_space=pltpu.VMEM)
    smem = pl.BlockSpec(memory_space=pltpu.SMEM)
    anywhere = pl.BlockSpec(memory_space=pl.ANY)
    bf16 = jnp.bfloat16
    dma = pltpu.SemaphoreType.DMA
    volt_shape, next_shape = (2, hl, block, snaps), (2, orders, conv, snaps)
    solved = pl.pallas_call(
        functools.partial(kernel, nh, ny),
        out_shape=(pltpu.VMEM(volt_shape, bf16), pltpu.VMEM(next_shape, bf16)),
        in_specs=[vmem, vmem, smem, smem, smem, vmem, vmem, vmem, vmem, vmem, vmem],
        out_specs=(vmem, vmem),
        scratch_shapes=[
            pltpu.VMEM((span, conv * LANES), bf16),
            pltpu.VMEM((nh, hl, 8, LANES), bf16),
            pltpu.VMEM((nh + 2, hl, 8, LANES), bf16),
            pltpu.VMEM((8, LANES), bf16),
            pltpu.VMEM((nh + 2, 8, LANES), bf16),
            pltpu.VMEM((2,) + admittance.shape[:3] + (LANES,), jnp.float32),
            pltpu.VMEM((2, link_offset.shape[0], LANES), jnp.int32),
            pltpu.VMEM((hl, tiles, 2 * LANES, 4 * LANES), bf16),
            pltpu.VMEM((hl, tiles, 8 * around + 2 * LANES, rows), bf16),
            pltpu.VMEM((nh, 2, hl, conv, LANES), bf16),
            dma((nh,)),
            dma((nh + 2,)),
            dma((nh,)),
            dma((nh,)),
            dma((nh,)),
            dma((nh + 2,)),
            dma((nh,)),
            dma((nh,)),
            dma((4,)),
            dma((4,)),
            dma((nh,)),
            dma((nh,)),
            dma,
        ],
        compiler_params=pltpu.CompilerParams(collective_id=0, has_side_effects=True, vmem_limit_bytes=56 * 2**20),
        name="power_flow",
    )(
        conv_volt.reshape(span * conv, snaps),
        conv_power,
        conv_type,
        type_steep,
        conv_bus,
        admittance,
        link_offset,
        jnp.asarray(basis.T, bf16),
        jnp.asarray(regrouped, bf16),
        jnp.asarray(perm, bf16),
        jnp.asarray(perm.T, bf16),
    )
    return pl.pallas_call(
        store,
        out_shape=(jax.ShapeDtypeStruct(volt_shape, bf16), jax.ShapeDtypeStruct(next_shape, bf16)),
        in_specs=[vmem, vmem],
        out_specs=(anywhere, anywhere),
        scratch_shapes=[dma((3,))],
        compiler_params=pltpu.CompilerParams(vmem_limit_bytes=32 * 2**20),
        name="store_results",
    )(*solved)


def solution(mesh):
    in_specs = (
        P(None, None, ("bus", "harm"), None),
        P(("bus", "harm"), None),
        P(("bus", "harm")),
        P(),
        P(("bus", "harm")),
        P(None, None, "harm", "bus"),
        P(None, "bus"),
    )
    out_specs = (P(None, "harm", "bus", None), P(None, None, ("bus", "harm"), None))
    body = functools.partial(local, mesh.shape["harm"], mesh.shape["bus"])
    return jax.shard_map(body, mesh=mesh, in_specs=in_specs, out_specs=out_specs, check_vma=False)
```

profile of v0, /device:TPU:0, one launch (start us, length us, event | category | flops | bytes accessed | tf_op | source)
XLA Modules:
  0.0 23.5 jit_solution(3851552196754448302)
XLA Ops:
  0.6 22.0 %power_flow.1 = (bf16[2,4,256,128]{3,2,1,0:T(8,128)(2,1)S(1)}, bf16[2,64,4,128]{3,2,1,0:T(4,128)(2,1)S(1)}) custom-call(bf16[512,128]{1,0:T(8,128)(2,1)} %bitcast.1, f32[4,128]{1,0:T(4,128)} %power_ref.1, s32[4]{0:T(128)} %type_ref.1, f32[8]{0:T(128)} %steep_ref.1, s32[4]{0:T(128)} %bus_ref.1, f32[2,4,4,256]{3,2,1,0:T(4,128)} %adm_ref.1, s32[3,256]{1,0:T(4,128)} %off_ref.1, ...), custom_call_target="tpu_custom_call" | custom-call | tf_op jit(solution)/shard_map/power_flow/pallas_call | solution.py:426
  22.7 0.9 %store_results.1 = (bf16[2,4,256,128]{3,2,1,0:T(8,128)(2,1)}, bf16[2,64,4,128]{3,2,1,0:T(4,128)(2,1)}) custom-call(bf16[2,4,256,128]{3,2,1,0:T(8,128)(2,1)S(1)} %get-tuple-element.4.volt_ref, bf16[2,64,4,128]{3,2,1,0:T(4,128)(2,1)S(1)} %get-tuple-element.5.next_ref), custom_call_target="tpu_custom_call" | custom-call | tf_op jit(solution)/shard_map/store_results/pallas_call | solution.py:471
where the time goes:
time: 23.7 us; the launch traced here: 23.5 us
  Pallas kernels  22.9 us (97%)
  between operations  0.64 us (3%)
    pallas_call x1, Pallas kernels, local(): pl.pallas_call(functools.partial(kernel, nh, ny), out_shape=(pltpu.VMEM(v...  22 us
    pallas_call x1, Pallas kernels, local(): pl.pallas_call(store, out_shape=(jax.ShapeDtypeStruct(volt_shape, bf16),...  0.86 us

commit v1 on v0

v1 whole, which is shorter than its diff:
```python
import functools
import math

import jax
import jax.numpy as jnp
import numpy as np
from jax import lax
from jax.experimental import pallas as pl
from jax.experimental.pallas import tpu as pltpu
from jax.sharding import PartitionSpec as P

NT = 1024
LANES = 128
CHUNKS = 4


def make_basis(orders):
    samples = np.arange(NT)
    phases = (np.arange(1, orders + 1)[:, None] * samples[None, :] % NT) * (2.0 * math.pi / NT)
    return np.concatenate([np.cos(phases), -np.sin(phases)], axis=0).astype(np.float32)


def kernel(
    nh,
    ny,
    volt_hbm,
    power_hbm,
    type_ref,
    steep_ref,
    bus_ref,
    adm_hbm,
    off_hbm,
    fwd_hbm,
    inv_hbm,
    out_ref,
    next_ref,
    volt_ref,
    power_ref,
    adm_ref,
    off_ref,
    fwd_ref,
    inv_ref,
    wide,
    volts,
    send,
    recv,
    my_bus,
    buses,
    adm_side,
    off_side,
    weights,
    resp,
    send_back,
    load_sem,
    send_sem,
    recv_sem,
):
    me = lax.axis_index("harm")
    y = lax.axis_index("bus")
    hl = adm_ref.shape[2]
    block = adm_ref.shape[3]
    links = off_ref.shape[0]
    conv = power_ref.shape[0]
    sub = block // nh
    tiles = block // LANES
    around = LANES // sub
    rows = 8 * (around + 2)
    has_left = y > 0
    has_right = y < ny - 1
    send_right = jnp.logical_and(has_right, me == nh - 1)
    send_left = jnp.logical_and(has_left, me == 0)

    pairs = (
        (volt_hbm, volt_ref),
        (fwd_hbm, fwd_ref),
        (power_hbm, power_ref),
        (inv_hbm, inv_ref),
        (adm_hbm, adm_ref),
        (off_hbm, off_ref),
    )
    loads = [pltpu.make_async_copy(src, dst, load_sem.at[i]) for i, (src, dst) in enumerate(pairs)]
    for load in loads:
        load.start()

    barrier = pltpu.get_barrier_semaphore()

    def greet(d, by):
        pl.semaphore_signal(barrier, inc=1, device_id={"harm": d, "bus": by})

    def each(low, body):
        def step(i, carry):
            body(i)
            return carry

        lax.fori_loop(low, nh, step, 0)

    def peer(s):
        return lax.rem(me + s, nh)

    each(1, lambda s: greet(peer(s), y))

    @pl.when(has_left)
    def _():
        each(0, lambda d: greet(d, y - 1))

    @pl.when(has_right)
    def _():
        each(0, lambda d: greet(d, y + 1))

    @pl.when(jnp.logical_not(has_left))
    def _():
        recv[0] = jnp.zeros(recv.shape[1:], recv.dtype)
        buses[0] = jnp.zeros(buses.shape[1:], buses.dtype)
        adm_side[0] = jnp.zeros(adm_side.shape[1:], adm_side.dtype)
        off_side[0] = jnp.zeros(off_side.shape[1:], off_side.dtype)

    @pl.when(jnp.logical_not(has_right))
    def _():
        recv[nh + 1] = jnp.zeros(recv.shape[1:], recv.dtype)
        buses[nh + 1] = jnp.zeros(buses.shape[1:], buses.dtype)
        adm_side[1] = jnp.zeros(adm_side.shape[1:], adm_side.dtype)
        off_side[1] = jnp.zeros(off_side.shape[1:], off_side.dtype)

    for load in loads[:4]:
        load.wait()
    span = volt_ref.shape[0] // conv
    wide[0 : span * conv] = volt_ref[...].astype(jnp.float32)
    for c in range(conv):
        volts[:, LANES * c : LANES * (c + 1)] = wide[pl.ds(c, span, stride=conv), :].astype(jnp.bfloat16)

    def steepness(c):
        value = steep_ref[0]
        for kind in range(1, steep_ref.shape[0]):
            value = jnp.where(type_ref[c] == kind, steep_ref[kind], value)
        return jnp.full((1, LANES), value, jnp.float32)

    steep = jnp.concatenate([steepness(c) for c in range(conv)], axis=1)
    power = jnp.concatenate([power_ref[c : c + 1, :] for c in range(conv)], axis=1) * NT ** (-0.5)
    part = NT // CHUNKS
    spectra = jnp.zeros((span, conv * LANES), jnp.float32)
    for q in range(CHUNKS):
        wave = jnp.dot(fwd_ref[part * q : part * (q + 1), :], volts[...], preferred_element_type=jnp.float32)
        now = jnp.tanh(steep * wave).astype(jnp.bfloat16)
        spectra = spectra + jnp.dot(
            inv_ref[:, part * q : part * (q + 1)], now, preferred_element_type=jnp.float32
        )
    spectra = spectra * power
    for c in range(conv):
        wide[pl.ds(c, span, stride=conv), :] = spectra[:, LANES * c : LANES * (c + 1)]
    send[...] = wide[0 : span * conv].reshape(nh, hl, 8, LANES).astype(jnp.bfloat16)

    for load in loads[4:]:
        load.wait()
    first = (y * nh + me) * sub
    row8 = lax.broadcasted_iota(jnp.int32, (8, LANES), 0) % conv
    numbers = jnp.zeros((8, LANES), jnp.float32)
    for c in range(conv):
        numbers = jnp.where(row8 == c, (bus_ref[c] - first).astype(jnp.float32), numbers)
    my_bus[...] = numbers.astype(jnp.bfloat16)

    pl.semaphore_wait(barrier, nh - 1 + nh * has_left.astype(jnp.int32) + nh * has_right.astype(jnp.int32))

    def remote(src, dst, out, into, d, by):
        return pltpu.make_async_remote_copy(
            src_ref=src,
            dst_ref=dst,
            send_sem=send_sem.at[out],
            recv_sem=recv_sem.at[into],
            device_id={"harm": d, "bus": by},
        )

    def bus_copy(d, slot, by, out, into):
        return remote(my_bus, buses.at[slot], out, into, d, by)

    def spec_copy(d, slot, by, out, into):
        return remote(send.at[d], recv.at[slot], out, into, d, by)

    def ret_copy(d, source):
        place = next_ref.at[:, pl.ds(source * hl, hl)]
        return remote(send_back.at[d], place, 6, 6, d, y)

    def side_copies(side):
        by = y + 1 if side == 0 else y - 1
        start = block - LANES if side == 0 else 0
        return (
            remote(adm_ref.at[:, :, :, pl.ds(start, LANES)], adm_side.at[side], 7 + side, 7 + side, me, by),
            remote(off_ref.at[:, pl.ds(start, LANES)], off_side.at[side], 9 + side, 9 + side, me, by),
        )

    each(1, lambda s: bus_copy(peer(s), me + 1, y, 0, 0).start())
    each(1, lambda s: spec_copy(peer(s), me + 1, y, 3, 3).start())

    @pl.when(send_right)
    def _():
        each(0, lambda d: bus_copy(d, 0, y + 1, 1, 1).start())
        each(0, lambda d: spec_copy(d, 0, y + 1, 4, 4).start())

    @pl.when(send_left)
    def _():
        each(0, lambda d: bus_copy(d, nh + 1, y - 1, 2, 2).start())
        each(0, lambda d: spec_copy(d, nh + 1, y - 1, 5, 5).start())

    @pl.when(has_right)
    def _():
        for copy in side_copies(0):
            copy.start()

    @pl.when(has_left)
    def _():
        for copy in side_copies(1):
            copy.start()

    recv[me + 1] = send[me]
    buses[me + 1] = my_bus[...]

    lane = lax.broadcasted_iota(jnp.int32, (1, LANES), 1)
    is_right = lane < LANES // 2

    def adm_row(p, k, h, t, beyond):
        def row_of(t):
            if t < 0:
                return adm_side[0, p, k, h : h + 1, :]
            if t >= tiles:
                return adm_side[1, p, k, h : h + 1, :]
            return adm_ref[p, k, h : h + 1, LANES * t : LANES * (t + 1)]

        return jnp.where(is_right, row_of(t + 1), row_of(t - 1)) if beyond else row_of(t)

    def off_row(k, t, beyond):
        def row_of(t):
            if t < 0:
                return off_side[0, k : k + 1, :]
            if t >= tiles:
                return off_side[1, k : k + 1, :]
            return off_ref[k : k + 1, LANES * t : LANES * (t + 1)]

        return jnp.where(is_right, row_of(t + 1), row_of(t - 1)) if beyond else row_of(t)

    def fill(t, beyond, low, high):
        band = lax.broadcasted_iota(jnp.int32, (high - low, LANES), 0) + low
        shift = LANES if beyond else 0
        masks = [
            band == jnp.bitwise_and(lane + shift + off_row(k, t, beyond), 2 * LANES - 1) for k in range(links)
        ]
        at = 2 * shift
        for h in range(hl):
            d_real, d_imag = adm_row(0, 0, h, t, beyond), adm_row(1, 0, h, t, beyond)
            total_real = jnp.zeros(band.shape, jnp.float32)
            total_imag = jnp.zeros(band.shape, jnp.float32)
            for k in range(links):
                l_real, l_imag = adm_row(0, 1 + k, h, t, beyond), adm_row(1, 1 + k, h, t, beyond)
                total_real += jnp.where(masks[k], d_real * l_real - d_imag * l_imag, 0.0)
                total_imag += jnp.where(masks[k], d_real * l_imag + d_imag * l_real, 0.0)
            weights[h, t, low:high, at : at + LANES] = total_real.astype(jnp.bfloat16)
            weights[h, t, low:high, at + LANES : at + 2 * LANES] = total_imag.astype(jnp.bfloat16)

    for t in range(tiles):
        fill(t, False, 0, LANES + 16)
        fill(t, False, 2 * LANES - 16, 2 * LANES)
        for h in range(hl):
            weights[h, t, LANES + 16 : 2 * LANES - 16, :] = jnp.zeros((LANES - 32, 4 * LANES), jnp.bfloat16)
            weights[h, t, 16 : LANES - 16, 2 * LANES :] = jnp.zeros((LANES - 32, 2 * LANES), jnp.bfloat16)

    @pl.when(has_left)
    def _():
        for copy in side_copies(0):
            copy.wait_recv()

    @pl.when(has_right)
    def _():
        for copy in side_copies(1):
            copy.wait_recv()

    for t in range(tiles):
        for low, high in ((LANES - 16, LANES + 16), (2 * LANES - 16, 2 * LANES), (0, 16)):
            fill(t, True, low, high)

    def all_of(ref, count, out, into):
        return remote(ref.at[pl.ds(0, count)], ref.at[pl.ds(0, count)], out, into, me, y)

    all_of(buses, nh - 1, 0, 0).wait_recv()

    @pl.when(has_left)
    def _():
        bus_copy(0, 0, y, 1, 1).wait_recv()

    @pl.when(has_right)
    def _():
        bus_copy(0, nh + 1, y, 2, 2).wait_recv()

    row = lax.broadcasted_iota(jnp.int32, (rows, LANES), 0)
    is_real = row % 8 < conv
    base = jnp.bitwise_and((row // 8 - 1) * sub, 2 * LANES - 1)
    own = 8 * around
    for t in range(tiles):
        near = buses[around * t : around * (t + 1) + 2].astype(jnp.float32).reshape(rows, LANES)
        at_bus = base + near.astype(jnp.int32)
        hits = [at_bus == lane, at_bus == lane + LANES]
        picked = jnp.where(hits[0], 1.0, 0.0)
        pick_real = jnp.where(is_real, picked, 0.0)[8 : 8 + own].astype(jnp.bfloat16)
        pick_imag = jnp.where(is_real, 0.0, picked)[8 : 8 + own].astype(jnp.bfloat16)
        for h in range(hl):
            start_real, start_imag = [], []
            for side in (False, True):
                d_real, d_imag = adm_row(0, 0, h, t, side), adm_row(1, 0, h, t, side)
                start_real.append(jnp.where(hits[side], jnp.where(is_real, d_real, -d_imag), 0.0))
                start_imag.append(jnp.where(hits[side], jnp.where(is_real, d_imag, d_real), 0.0))
            now_real, now_imag = start_real, start_imag
            for last in (False, True):
                state = jnp.concatenate(
                    [jnp.concatenate(now_real, axis=1), jnp.concatenate(now_imag, axis=1)], axis=0
                ).astype(jnp.bfloat16)
                width = 2 * LANES if last else 4 * LANES
                both = jnp.dot(state, weights[h, t, :, 0:width], preferred_element_type=jnp.float32)
                new_real, new_imag = [], []
                for a in range(1 if last else 2):
                    at = 2 * LANES * a
                    left, right = both[:, at : at + LANES], both[:, at + LANES : at + 2 * LANES]
                    new_real.append(start_real[a] + left[:rows] - right[rows:])
                    new_imag.append(start_imag[a] + right[:rows] + left[rows:])
                now_real, now_imag = new_real, new_imag
            real_t = now_real[0].T.astype(jnp.bfloat16)
            imag_t = now_imag[0].T.astype(jnp.bfloat16)
            resp[h, t, own : own + LANES, :] = real_t
            resp[h, t, own + LANES :, :] = imag_t
            chosen = jnp.dot(pick_real, real_t, preferred_element_type=jnp.float32)
            chosen += jnp.dot(pick_imag, imag_t, preferred_element_type=jnp.float32)
            resp[h, t, 0:own, :] = chosen.astype(jnp.bfloat16)

    all_of(recv, nh - 1, 3, 3).wait_recv()

    @pl.when(has_left)
    def _():
        spec_copy(0, 0, y, 4, 4).wait_recv()

    @pl.when(has_right)
    def _():
        spec_copy(0, nh + 1, y, 5, 5).wait_recv()

    arrived = []
    for t in range(tiles):
        for h in range(hl):
            here = recv[around * t : around * (t + 1) + 2, h].astype(jnp.float32)
            arrived.append(here.reshape(rows, LANES).astype(jnp.bfloat16))
            at_conv = jnp.dot(resp[h, t, 0:own, :], arrived[-1], preferred_element_type=jnp.float32)
            at_conv = at_conv.reshape(around, 2, conv, LANES).astype(jnp.bfloat16)
            send_back[around * t : around * (t + 1), :, h] = at_conv
    each(1, lambda s: ret_copy(peer(s), me).start())
    next_ref[:, pl.ds(me * hl, hl)] = send_back[me]
    for t in range(tiles):
        for h in range(hl):
            solved = jnp.dot(resp[h, t, own:, :], arrived[t * hl + h], preferred_element_type=jnp.float32)
            out_ref[:, h, LANES * t : LANES * (t + 1)] = solved.astype(jnp.bfloat16).reshape(2, LANES, LANES)

    all_of(buses, nh - 1, 0, 0).wait_send()
    all_of(recv, nh - 1, 3, 3).wait_send()

    @pl.when(has_right)
    def _():
        for copy in side_copies(0):
            copy.wait_send()

    @pl.when(has_left)
    def _():
        for copy in side_copies(1):
            copy.wait_send()

    @pl.when(send_right)
    def _():
        all_of(buses, nh, 1, 1).wait_send()
        all_of(recv, nh, 4, 4).wait_send()

    @pl.when(send_left)
    def _():
        all_of(buses, nh, 2, 2).wait_send()
        all_of(recv, nh, 5, 5).wait_send()

    all_of(send_back, nh - 1, 6, 6).wait_send()
    all_of(send_back, nh - 1, 6, 6).wait_recv()


def store(volt_ref, next_ref, volt_out, next_out, sems):
    copies = [pltpu.make_async_copy(volt_ref.at[p], volt_out.at[p], sems.at[p]) for p in range(2)]
    copies.append(pltpu.make_async_copy(next_ref, next_out, sems.at[2]))
    for copy in copies:
        copy.start()
    for copy in copies:
        copy.wait()


def local(nh, ny, conv_volt, conv_power, conv_type, type_steep, conv_bus, admittance, link_offset):
    _, orders, conv, snaps = conv_volt.shape
    hl = orders // nh
    block = admittance.shape[3]
    tiles = block // LANES
    around = LANES * nh // block
    rows = 8 * (around + 2)
    span = 2 * orders
    basis = make_basis(orders)
    regrouped = basis.reshape(2, orders, NT).transpose(1, 0, 2).reshape(span, NT)
    vmem = pl.BlockSpec(memory_space=pltpu.VMEM)
    smem = pl.BlockSpec(memory_space=pltpu.SMEM)
    anywhere = pl.BlockSpec(memory_space=pl.ANY)
    bf16 = jnp.bfloat16
    dma = pltpu.SemaphoreType.DMA
    volt_shape, next_shape = (2, hl, block, snaps), (2, orders, conv, snaps)
    solved = pl.pallas_call(
        functools.partial(kernel, nh, ny),
        out_shape=(pltpu.VMEM(volt_shape, bf16), pltpu.VMEM(next_shape, bf16)),
        in_specs=[anywhere, anywhere, smem, smem, smem, anywhere, anywhere, anywhere, anywhere],
        out_specs=(vmem, vmem),
        scratch_shapes=[
            pltpu.VMEM((span * conv, snaps), bf16),
            pltpu.VMEM((conv, snaps), jnp.float32),
            pltpu.VMEM(admittance.shape, jnp.float32),
            pltpu.VMEM(link_offset.shape, jnp.int32),
            pltpu.VMEM((NT, span), bf16),
            pltpu.VMEM((span, NT), bf16),
            pltpu.VMEM((span * conv + 8, LANES), jnp.float32),
            pltpu.VMEM((span, conv * LANES), bf16),
            pltpu.VMEM((nh, hl, 8, LANES), bf16),
            pltpu.VMEM((nh + 2, hl, 8, LANES), bf16),
            pltpu.VMEM((8, LANES), bf16),
            pltpu.VMEM((nh + 2, 8, LANES), bf16),
            pltpu.VMEM((2,) + admittance.shape[:3] + (LANES,), jnp.float32),
            pltpu.VMEM((2, link_offset.shape[0], LANES), jnp.int32),
            pltpu.VMEM((hl, tiles, 2 * LANES, 4 * LANES), bf16),
            pltpu.VMEM((hl, tiles, 8 * around + 2 * LANES, rows), bf16),
            pltpu.VMEM((nh, 2, hl, conv, LANES), bf16),
            dma((6,)),
            dma((11,)),
            dma((11,)),
        ],
        compiler_params=pltpu.CompilerParams(collective_id=0, has_side_effects=True, vmem_limit_bytes=56 * 2**20),
        name="power_flow",
    )(
        conv_volt.reshape(span * conv, snaps),
        conv_power,
        conv_type,
        type_steep,
        conv_bus,
        admittance,
        link_offset,
        jnp.asarray(basis.T, bf16),
        jnp.asarray(regrouped, bf16),
    )
    return pl.pallas_call(
        store,
        out_shape=(jax.ShapeDtypeStruct(volt_shape, bf16), jax.ShapeDtypeStruct(next_shape, bf16)),
        in_specs=[vmem, vmem],
        out_specs=(anywhere, anywhere),
        scratch_shapes=[dma((3,))],
        compiler_params=pltpu.CompilerParams(vmem_limit_bytes=32 * 2**20),
        name="store_results",
    )(*solved)


def solution(mesh):
    in_specs = (
        P(None, None, ("bus", "harm"), None),
        P(("bus", "harm"), None),
        P(("bus", "harm")),
        P(),
        P(("bus", "harm")),
        P(None, None, "harm", "bus"),
        P(None, "bus"),
    )
    out_specs = (P(None, "harm", "bus", None), P(None, None, ("bus", "harm"), None))
    body = functools.partial(local, mesh.shape["harm"], mesh.shape["bus"])
    return jax.shard_map(body, mesh=mesh, in_specs=in_specs, out_specs=out_specs, check_vma=False)
```

time: 23.7 us -> 23.6 us (level)
  no operation moved by 1% of the time
where the time goes in v1:
time: 23.6 us; the launch traced here: 23.4 us
  Pallas kernels  22.8 us (97%)
  between operations  0.64 us (3%)
    pallas_call x1, Pallas kernels, local(): pl.pallas_call(functools.partial(kernel, nh, ny), out_shape=(pltpu.VMEM(v...  21.9 us
    pallas_call x1, Pallas kernels, local(): pl.pallas_call(store, out_shape=(jax.ShapeDtypeStruct(volt_shape, bf16),...  0.86 us

profile of v1, /device:TPU:0, one launch (start us, length us, event | category | flops | bytes accessed | tf_op | source)
XLA Modules:
  0.0 23.4 jit_solution(16708318523519306596)
XLA Ops:
  0.6 21.9 %power_flow.1 = (bf16[2,4,256,128]{3,2,1,0:T(8,128)(2,1)S(1)}, bf16[2,64,4,128]{3,2,1,0:T(4,128)(2,1)S(1)}) custom-call(bf16[512,128]{1,0:T(8,128)(2,1)} %bitcast.1, f32[4,128]{1,0:T(4,128)} %power_hbm.1, s32[4]{0:T(128)} %type_ref.1, f32[8]{0:T(128)} %steep_ref.1, s32[4]{0:T(128)} %bus_ref.1, f32[2,4,4,256]{3,2,1,0:T(4,128)} %adm_hbm.1, s32[3,256]{1,0:T(4,128)} %off_hbm.1, ...), custom_call_target="tpu_custom_call" | custom-call | tf_op jit(solution)/shard_map/power_flow/pallas_call | solution.py:407
  22.5 0.9 %store_results.1 = (bf16[2,4,256,128]{3,2,1,0:T(8,128)(2,1)}, bf16[2,64,4,128]{3,2,1,0:T(4,128)(2,1)}) custom-call(bf16[2,4,256,128]{3,2,1,0:T(8,128)(2,1)S(1)} %get-tuple-element.4.volt_ref, bf16[2,64,4,128]{3,2,1,0:T(4,128)(2,1)S(1)} %get-tuple-element.5.next_ref), custom_call_target="tpu_custom_call" | custom-call | tf_op jit(solution)/shard_map/store_results/pallas_call | solution.py:447

commit v2 on v1

--- a/solution.py
+++ b/solution.py
@@ -25,9 +25,9 @@
     ny,
     volt_hbm,
     power_hbm,
-    type_ref,
-    steep_ref,
-    bus_ref,
+    type_hbm,
+    steep_hbm,
+    bus_hbm,
     adm_hbm,
     off_hbm,
     fwd_hbm,
@@ -35,7 +35,10 @@
     out_ref,
     next_ref,
     volt_ref,
+    type_ref,
+    steep_ref,
     power_ref,
+    bus_ref,
     adm_ref,
     off_ref,
     fwd_ref,
@@ -73,8 +76,11 @@
     pairs = (
         (volt_hbm, volt_ref),
         (fwd_hbm, fwd_ref),
+        (type_hbm, type_ref),
+        (steep_hbm, steep_ref),
         (power_hbm, power_ref),
         (inv_hbm, inv_ref),
+        (bus_hbm, bus_ref),
         (adm_hbm, adm_ref),
         (off_hbm, off_ref),
     )
@@ -121,7 +127,7 @@
         adm_side[1] = jnp.zeros(adm_side.shape[1:], adm_side.dtype)
         off_side[1] = jnp.zeros(off_side.shape[1:], off_side.dtype)
 
-    for load in loads[:4]:
+    for load in loads[:6]:
         load.wait()
     span = volt_ref.shape[0] // conv
     wide[0 : span * conv] = volt_ref[...].astype(jnp.float32)
@@ -149,7 +155,7 @@
         wide[pl.ds(c, span, stride=conv), :] = spectra[:, LANES * c : LANES * (c + 1)]
     send[...] = wide[0 : span * conv].reshape(nh, hl, 8, LANES).astype(jnp.bfloat16)
 
-    for load in loads[4:]:
+    for load in loads[6:]:
         load.wait()
     first = (y * nh + me) * sub
     row8 = lax.broadcasted_iota(jnp.int32, (8, LANES), 0) % conv
@@ -187,6 +193,16 @@
             remote(off_ref.at[:, pl.ds(start, LANES)], off_side.at[side], 9 + side, 9 + side, me, by),
         )
 
+    @pl.when(has_right)
+    def _():
+        for copy in side_copies(0):
+            copy.start()
+
+    @pl.when(has_left)
+    def _():
+        for copy in side_copies(1):
+            copy.start()
+
     each(1, lambda s: bus_copy(peer(s), me + 1, y, 0, 0).start())
     each(1, lambda s: spec_copy(peer(s), me + 1, y, 3, 3).start())
 
@@ -199,16 +215,6 @@
     def _():
         each(0, lambda d: bus_copy(d, nh + 1, y - 1, 2, 2).start())
         each(0, lambda d: spec_copy(d, nh + 1, y - 1, 5, 5).start())
-
-    @pl.when(has_right)
-    def _():
-        for copy in side_copies(0):
-            copy.start()
-
-    @pl.when(has_left)
-    def _():
-        for copy in side_copies(1):
-            copy.start()
 
     recv[me + 1] = send[me]
     buses[me + 1] = my_bus[...]
@@ -242,7 +248,6 @@
         masks = [
             band == jnp.bitwise_and(lane + shift + off_row(k, t, beyond), 2 * LANES - 1) for k in range(links)
         ]
-        at = 2 * shift
         for h in range(hl):
             d_real, d_imag = adm_row(0, 0, h, t, beyond), adm_row(1, 0, h, t, beyond)
             total_real = jnp.zeros(band.shape, jnp.float32)
@@ -251,15 +256,16 @@
                 l_real, l_imag = adm_row(0, 1 + k, h, t, beyond), adm_row(1, 1 + k, h, t, beyond)
                 total_real += jnp.where(masks[k], d_real * l_real - d_imag * l_imag, 0.0)
                 total_imag += jnp.where(masks[k], d_real * l_imag + d_imag * l_real, 0.0)
-            weights[h, t, low:high, at : at + LANES] = total_real.astype(jnp.bfloat16)
-            weights[h, t, low:high, at + LANES : at + 2 * LANES] = total_imag.astype(jnp.bfloat16)
+            weights[h, t, low:high, shift : shift + LANES] = total_real.astype(jnp.bfloat16)
+            weights[h, t, low:high, shift + 2 * LANES : shift + 3 * LANES] = total_imag.astype(jnp.bfloat16)
 
     for t in range(tiles):
         fill(t, False, 0, LANES + 16)
         fill(t, False, 2 * LANES - 16, 2 * LANES)
         for h in range(hl):
             weights[h, t, LANES + 16 : 2 * LANES - 16, :] = jnp.zeros((LANES - 32, 4 * LANES), jnp.bfloat16)
-            weights[h, t, 16 : LANES - 16, 2 * LANES :] = jnp.zeros((LANES - 32, 2 * LANES), jnp.bfloat16)
+            for at in (LANES, 3 * LANES):
+                weights[h, t, 16 : LANES - 16, at : at + LANES] = jnp.zeros((LANES - 32, LANES), jnp.bfloat16)
 
     @pl.when(has_left)
     def _():
@@ -277,6 +283,30 @@
 
     def all_of(ref, count, out, into):
         return remote(ref.at[pl.ds(0, count)], ref.at[pl.ds(0, count)], out, into, me, y)
+
+    across = (((1,), (1,)), ((), ()))
+    eye = jnp.where(lax.broadcasted_iota(jnp.int32, (LANES, LANES), 0) == lane, 1.0, 0.0)
+    unit = jnp.concatenate([eye, jnp.zeros((LANES, LANES), jnp.float32)], axis=1)
+    for t in range(tiles):
+        for h in range(hl):
+            own = jnp.concatenate(
+                [weights[h, t, :, 0:LANES], weights[h, t, :, 2 * LANES : 3 * LANES]], axis=0
+            )
+            flipped = lax.dot_general(eye.astype(jnp.bfloat16), own, across, preferred_element_type=jnp.float32)
+            step = jnp.concatenate([unit + flipped[:, : 2 * LANES], flipped[:, 2 * LANES :]], axis=0)
+            step = step.astype(jnp.bfloat16)
+            by_real = lax.dot_general(
+                step, weights[h, t, :, 0 : 2 * LANES], across, preferred_element_type=jnp.float32
+            )
+            by_imag = lax.dot_general(
+                step, weights[h, t, :, 2 * LANES :], across, preferred_element_type=jnp.float32
+            )
+            real = unit + by_real[:LANES] - by_imag[LANES:]
+            imag = by_imag[:LANES] + by_real[LANES:]
+            d_real = jnp.concatenate([adm_row(0, 0, h, t, False), adm_row(0, 0, h, t, True)], axis=1)
+            d_imag = jnp.concatenate([adm_row(1, 0, h, t, False), adm_row(1, 0, h, t, True)], axis=1)
+            resp[h, t, 0:LANES] = (real * d_real - imag * d_imag).astype(jnp.bfloat16)
+            resp[h, t, LANES:] = (real * d_imag + imag * d_real).astype(jnp.bfloat16)
 
     all_of(buses, nh - 1, 0, 0).wait_recv()
 
@@ -292,40 +322,14 @@
     is_real = row % 8 < conv
     base = jnp.bitwise_and((row // 8 - 1) * sub, 2 * LANES - 1)
     own = 8 * around
+    spread, gather = [], []
     for t in range(tiles):
         near = buses[around * t : around * (t + 1) + 2].astype(jnp.float32).reshape(rows, LANES)
         at_bus = base + near.astype(jnp.int32)
-        hits = [at_bus == lane, at_bus == lane + LANES]
-        picked = jnp.where(hits[0], 1.0, 0.0)
-        pick_real = jnp.where(is_real, picked, 0.0)[8 : 8 + own].astype(jnp.bfloat16)
-        pick_imag = jnp.where(is_real, 0.0, picked)[8 : 8 + own].astype(jnp.bfloat16)
-        for h in range(hl):
-            start_real, start_imag = [], []
-            for side in (False, True):
-                d_real, d_imag = adm_row(0, 0, h, t, side), adm_row(1, 0, h, t, side)
-                start_real.append(jnp.where(hits[side], jnp.where(is_real, d_real, -d_imag), 0.0))
-                start_imag.append(jnp.where(hits[side], jnp.where(is_real, d_imag, d_real), 0.0))
-            now_real, now_imag = start_real, start_imag
-            for last in (False, True):
-                state = jnp.concatenate(
-                    [jnp.concatenate(now_real, axis=1), jnp.concatenate(now_imag, axis=1)], axis=0
-                ).astype(jnp.bfloat16)
-                width = 2 * LANES if last else 4 * LANES
-                both = jnp.dot(state, weights[h, t, :, 0:width], preferred_element_type=jnp.float32)
-                new_real, new_imag = [], []
-                for a in range(1 if last else 2):
-                    at = 2 * LANES * a
-                    left, right = both[:, at : at + LANES], both[:, at + LANES : at + 2 * LANES]
-                    new_real.append(start_real[a] + left[:rows] - right[rows:])
-                    new_imag.append(start_imag[a] + right[:rows] + left[rows:])
-                now_real, now_imag = new_real, new_imag
-            real_t = now_real[0].T.astype(jnp.bfloat16)
-            imag_t = now_imag[0].T.astype(jnp.bfloat16)
-            resp[h, t, own : own + LANES, :] = real_t
-            resp[h, t, own + LANES :, :] = imag_t
-            chosen = jnp.dot(pick_real, real_t, preferred_element_type=jnp.float32)
-            chosen += jnp.dot(pick_imag, imag_t, preferred_element_type=jnp.float32)
-            resp[h, t, 0:own, :] = chosen.astype(jnp.bfloat16)
+        hits = [jnp.where(at_bus == lane + shift, 1.0, 0.0) for shift in (0, LANES)]
+        spread.append(jnp.concatenate([hit.T for hit in hits], axis=0).astype(jnp.bfloat16))
+        picks = [jnp.where(is_real, hits[0], 0.0), jnp.where(is_real, 0.0, hits[0])]
+        gather.append(jnp.concatenate(picks, axis=1)[8 : 8 + own].astype(jnp.bfloat16))
 
     all_of(recv, nh - 1, 3, 3).wait_recv()
 
@@ -337,20 +341,21 @@
     def _():
         spec_copy(0, nh + 1, y, 5, 5).wait_recv()
 
-    arrived = []
     for t in range(tiles):
         for h in range(hl):
-            here = recv[around * t : around * (t + 1) + 2, h].astype(jnp.float32)
-            arrived.append(here.reshape(rows, LANES).astype(jnp.bfloat16))
-            at_conv = jnp.dot(resp[h, t, 0:own, :], arrived[-1], preferred_element_type=jnp.float32)
+            here = recv[around * t : around * (t + 1) + 2, h].astype(jnp.float32).reshape(rows, LANES)
+            parts = jnp.concatenate([jnp.where(is_real, here, 0.0), jnp.where(is_real, 0.0, here)], axis=1)
+            injected = jnp.dot(spread[t], parts.astype(jnp.bfloat16), preferred_element_type=jnp.float32)
+            solved = jnp.dot(resp[h, t], injected.astype(jnp.bfloat16), preferred_element_type=jnp.float32)
+            real = solved[:LANES, :LANES] - solved[LANES:, LANES:]
+            imag = solved[:LANES, LANES:] + solved[LANES:, :LANES]
+            volt = jnp.concatenate([real, imag], axis=0).astype(jnp.bfloat16)
+            out_ref[:, h, LANES * t : LANES * (t + 1)] = volt.reshape(2, LANES, LANES)
+            at_conv = jnp.dot(gather[t], volt, preferred_element_type=jnp.float32)
             at_conv = at_conv.reshape(around, 2, conv, LANES).astype(jnp.bfloat16)
             send_back[around * t : around * (t + 1), :, h] = at_conv
     each(1, lambda s: ret_copy(peer(s), me).start())
     next_ref[:, pl.ds(me * hl, hl)] = send_back[me]
-    for t in range(tiles):
-        for h in range(hl):
-            solved = jnp.dot(resp[h, t, own:, :], arrived[t * hl + h], preferred_element_type=jnp.float32)
-            out_ref[:, h, LANES * t : LANES * (t + 1)] = solved.astype(jnp.bfloat16).reshape(2, LANES, LANES)
 
     all_of(buses, nh - 1, 0, 0).wait_send()
     all_of(recv, nh - 1, 3, 3).wait_send()
@@ -394,12 +399,10 @@
     block = admittance.shape[3]
     tiles = block // LANES
     around = LANES * nh // block
-    rows = 8 * (around + 2)
     span = 2 * orders
     basis = make_basis(orders)
     regrouped = basis.reshape(2, orders, NT).transpose(1, 0, 2).reshape(span, NT)
     vmem = pl.BlockSpec(memory_space=pltpu.VMEM)
-    smem = pl.BlockSpec(memory_space=pltpu.SMEM)
     anywhere = pl.BlockSpec(memory_space=pl.ANY)
     bf16 = jnp.bfloat16
     dma = pltpu.SemaphoreType.DMA
@@ -407,11 +410,14 @@
     solved = pl.pallas_call(
         functools.partial(kernel, nh, ny),
         out_shape=(pltpu.VMEM(volt_shape, bf16), pltpu.VMEM(next_shape, bf16)),
-        in_specs=[anywhere, anywhere, smem, smem, smem, anywhere, anywhere, anywhere, anywhere],
+        in_specs=[anywhere] * 9,
         out_specs=(vmem, vmem),
         scratch_shapes=[
             pltpu.VMEM((span * conv, snaps), bf16),
+            pltpu.SMEM(conv_type.shape, jnp.int32),
+            pltpu.SMEM(type_steep.shape, jnp.float32),
             pltpu.VMEM((conv, snaps), jnp.float32),
+            pltpu.SMEM(conv_bus.shape, jnp.int32),
             pltpu.VMEM(admittance.shape, jnp.float32),
             pltpu.VMEM(link_offset.shape, jnp.int32),
             pltpu.VMEM((NT, span), bf16),
@@ -425,9 +431,9 @@
             pltpu.VMEM((2,) + admittance.shape[:3] + (LANES,), jnp.float32),
             pltpu.VMEM((2, link_offset.shape[0], LANES), jnp.int32),
             pltpu.VMEM((hl, tiles, 2 * LANES, 4 * LANES), bf16),
-            pltpu.VMEM((hl, tiles, 8 * around + 2 * LANES, rows), bf16),
+            pltpu.VMEM((hl, tiles, 2 * LANES, 2 * LANES), bf16),
             pltpu.VMEM((nh, 2, hl, conv, LANES), bf16),
-            dma((6,)),
+            dma((9,)),
             dma((11,)),
             dma((11,)),
         ],

time: 23.6 us -> 23.3 us (0.987)
  Pallas kernels: 22.8 us -> 22.5 us
where the time goes in v2:
time: 23.3 us; the launch traced here: 23.2 us
  Pallas kernels  22.5 us (97%)
  between operations  0.64 us (3%)
    pallas_call x1, Pallas kernels, local(): pl.pallas_call(functools.partial(kernel, nh, ny), out_shape=(pltpu.VMEM(v...  21.7 us
    pallas_call x1, Pallas kernels, local(): pl.pallas_call(store, out_shape=(jax.ShapeDtypeStruct(volt_shape, bf16),...  0.86 us

profile of v2, /device:TPU:0, one launch (start us, length us, event | category | flops | bytes accessed | tf_op | source)
XLA Modules:
  0.0 23.2 jit_solution(12797270421640190516)
XLA Ops:
  0.6 21.7 %power_flow.1 = (bf16[2,4,256,128]{3,2,1,0:T(8,128)(2,1)S(1)}, bf16[2,64,4,128]{3,2,1,0:T(4,128)(2,1)S(1)}) custom-call(bf16[512,128]{1,0:T(8,128)(2,1)} %bitcast.1, f32[4,128]{1,0:T(4,128)} %power_hbm.1, s32[4]{0:T(128)} %type_hbm.1, f32[8]{0:T(128)} %steep_hbm.1, s32[4]{0:T(128)} %bus_hbm.1, f32[2,4,4,256]{3,2,1,0:T(4,128)} %adm_hbm.1, s32[3,256]{1,0:T(4,128)} %off_hbm.1, ...), custom_call_target="tpu_custom_call" | custom-call | tf_op jit(solution)/shard_map/power_flow/pallas_call | solution.py:410
  22.3 0.9 %store_results.1 = (bf16[2,4,256,128]{3,2,1,0:T(8,128)(2,1)}, bf16[2,64,4,128]{3,2,1,0:T(4,128)(2,1)}) custom-call(bf16[2,4,256,128]{3,2,1,0:T(8,128)(2,1)S(1)} %get-tuple-element.4.volt_ref, bf16[2,64,4,128]{3,2,1,0:T(4,128)(2,1)S(1)} %get-tuple-element.5.next_ref), custom_call_target="tpu_custom_call" | custom-call | tf_op jit(solution)/shard_map/store_results/pallas_call | solution.py:453

commit v3 on v2

--- a/solution.py
+++ b/solution.py
@@ -341,21 +341,35 @@
     def _():
         spec_copy(0, nh + 1, y, 5, 5).wait_recv()
 
-    for t in range(tiles):
+    injected, solved, volts_now = [], [], []
+    for t in range(tiles):
+        parts = []
         for h in range(hl):
             here = recv[around * t : around * (t + 1) + 2, h].astype(jnp.float32).reshape(rows, LANES)
-            parts = jnp.concatenate([jnp.where(is_real, here, 0.0), jnp.where(is_real, 0.0, here)], axis=1)
-            injected = jnp.dot(spread[t], parts.astype(jnp.bfloat16), preferred_element_type=jnp.float32)
-            solved = jnp.dot(resp[h, t], injected.astype(jnp.bfloat16), preferred_element_type=jnp.float32)
-            real = solved[:LANES, :LANES] - solved[LANES:, LANES:]
-            imag = solved[:LANES, LANES:] + solved[LANES:, :LANES]
-            volt = jnp.concatenate([real, imag], axis=0).astype(jnp.bfloat16)
-            out_ref[:, h, LANES * t : LANES * (t + 1)] = volt.reshape(2, LANES, LANES)
-            at_conv = jnp.dot(gather[t], volt, preferred_element_type=jnp.float32)
-            at_conv = at_conv.reshape(around, 2, conv, LANES).astype(jnp.bfloat16)
-            send_back[around * t : around * (t + 1), :, h] = at_conv
+            parts += [jnp.where(is_real, here, 0.0), jnp.where(is_real, 0.0, here)]
+        parts = jnp.concatenate(parts, axis=1).astype(jnp.bfloat16)
+        injected.append(jnp.dot(spread[t], parts, preferred_element_type=jnp.float32).astype(jnp.bfloat16))
+    for t in range(tiles):
+        for h in range(hl):
+            mine = injected[t][:, 2 * LANES * h : 2 * LANES * (h + 1)]
+            solved.append(jnp.dot(resp[h, t], mine, preferred_element_type=jnp.float32))
+    for t in range(tiles):
+        now = []
+        for h in range(hl):
+            both = solved[t * hl + h]
+            real = both[:LANES, :LANES] - both[LANES:, LANES:]
+            imag = both[:LANES, LANES:] + both[LANES:, :LANES]
+            now.append(jnp.concatenate([real, imag], axis=0).astype(jnp.bfloat16))
+        volts_now.append(now)
+        at_conv = jnp.dot(gather[t], jnp.concatenate(now, axis=1), preferred_element_type=jnp.float32)
+        for h in range(hl):
+            chosen = at_conv[:, LANES * h : LANES * (h + 1)].reshape(around, 2, conv, LANES)
+            send_back[around * t : around * (t + 1), :, h] = chosen.astype(jnp.bfloat16)
     each(1, lambda s: ret_copy(peer(s), me).start())
     next_ref[:, pl.ds(me * hl, hl)] = send_back[me]
+    for t in range(tiles):
+        for h in range(hl):
+            out_ref[:, h, LANES * t : LANES * (t + 1)] = volts_now[t][h].reshape(2, LANES, LANES)
 
     all_of(buses, nh - 1, 0, 0).wait_send()
     all_of(recv, nh - 1, 3, 3).wait_send()

time: 23.3 us -> 21.4 us (0.918)
  Pallas kernels: 22.5 us -> 20.6 us
    pallas_call x1, Pallas kernels: 21.7 us -> 19.8 us  [local(): pl.pallas_call(functools.partial(kernel, nh, ny), out_shape=(pltpu.VMEM(v...]
where the time goes in v3:
time: 21.4 us; the launch traced here: 21.3 us
  Pallas kernels  20.6 us (96%)
  between operations  0.64 us (3%)
    pallas_call x1, Pallas kernels, local(): pl.pallas_call(functools.partial(kernel, nh, ny), out_shape=(pltpu.VMEM(v...  19.8 us
    pallas_call x1, Pallas kernels, local(): pl.pallas_call(store, out_shape=(jax.ShapeDtypeStruct(volt_shape, bf16),...  0.86 us

profile of v3, /device:TPU:0, one launch (start us, length us, event | category | flops | bytes accessed | tf_op | source)
XLA Modules:
  0.0 21.3 jit_solution(1787896259613957820)
XLA Ops:
  0.6 19.8 %power_flow.1 = (bf16[2,4,256,128]{3,2,1,0:T(8,128)(2,1)S(1)}, bf16[2,64,4,128]{3,2,1,0:T(4,128)(2,1)S(1)}) custom-call(bf16[512,128]{1,0:T(8,128)(2,1)} %bitcast.1, f32[4,128]{1,0:T(4,128)} %power_hbm.1, s32[4]{0:T(128)} %type_hbm.1, f32[8]{0:T(128)} %steep_hbm.1, s32[4]{0:T(128)} %bus_hbm.1, f32[2,4,4,256]{3,2,1,0:T(4,128)} %adm_hbm.1, s32[3,256]{1,0:T(4,128)} %off_hbm.1, ...), custom_call_target="tpu_custom_call" | custom-call | tf_op jit(solution)/shard_map/power_flow/pallas_call | solution.py:424
  20.4 0.9 %store_results.1 = (bf16[2,4,256,128]{3,2,1,0:T(8,128)(2,1)}, bf16[2,64,4,128]{3,2,1,0:T(4,128)(2,1)}) custom-call(bf16[2,4,256,128]{3,2,1,0:T(8,128)(2,1)S(1)} %get-tuple-element.4.volt_ref, bf16[2,64,4,128]{3,2,1,0:T(4,128)(2,1)S(1)} %get-tuple-element.5.next_ref), custom_call_target="tpu_custom_call" | custom-call | tf_op jit(solution)/shard_map/store_results/pallas_call | solution.py:467

commit v4 on v3

--- a/solution.py
+++ b/solution.py
@@ -11,6 +11,7 @@
 
 NT = 1024
 LANES = 128
+REACH = 8
 CHUNKS = 4
 
 
@@ -53,7 +54,11 @@
     off_side,
     weights,
     resp,
-    send_back,
+    parcels,
+    parcel_recv,
+    parcel_edge,
+    near_spec,
+    off_row8,
     load_sem,
     send_sem,
     recv_sem,
@@ -68,8 +73,12 @@
     tiles = block // LANES
     around = LANES // sub
     rows = 8 * (around + 2)
+    deep = parcels.shape[1] // 4
+    inner, outer = sub + 2 * REACH, sub + 4 * REACH
     has_left = y > 0
     has_right = y < ny - 1
+    place = y * nh + me
+    near_left, near_right = place > 0, place < ny * nh - 1
     send_right = jnp.logical_and(has_right, me == nh - 1)
     send_left = jnp.logical_and(has_left, me == 0)
 
@@ -127,6 +136,18 @@
         adm_side[1] = jnp.zeros(adm_side.shape[1:], adm_side.dtype)
         off_side[1] = jnp.zeros(off_side.shape[1:], off_side.dtype)
 
+    @pl.when(jnp.logical_not(jnp.logical_or(send_left, send_right)))
+    def _():
+        parcel_edge[...] = jnp.zeros(parcel_edge.shape, parcel_edge.dtype)
+
+    @pl.when(jnp.logical_not(near_left))
+    def _():
+        near_spec[0] = jnp.zeros(near_spec.shape[1:], near_spec.dtype)
+
+    @pl.when(jnp.logical_not(near_right))
+    def _():
+        near_spec[1] = jnp.zeros(near_spec.shape[1:], near_spec.dtype)
+
     for load in loads[:6]:
         load.wait()
     span = volt_ref.shape[0] // conv
@@ -164,6 +185,41 @@
         numbers = jnp.where(row8 == c, (bus_ref[c] - first).astype(jnp.float32), numbers)
     my_bus[...] = numbers.astype(jnp.bfloat16)
 
+    lane = lax.broadcasted_iota(jnp.int32, (1, LANES), 1)
+
+    def window(pieces, start, at):
+        first_piece = start // LANES
+        shift = (at - start) % LANES
+        moved = []
+        for piece in (first_piece, first_piece + 1):
+            if 0 <= piece < len(pieces):
+                moved.append(pltpu.roll(pieces[piece], shift, 1) if shift else pieces[piece])
+            else:
+                moved.append(jnp.zeros(pieces[0].shape, pieces[0].dtype))
+        return jnp.where(lane - at < LANES * (first_piece + 1) - start, moved[0], moved[1])
+
+    def stacked(real, imag):
+        if deep == hl:
+            return jnp.concatenate([real, imag], axis=0)
+        empty = jnp.zeros((deep - hl, LANES), jnp.float32)
+        return jnp.concatenate([real, empty, imag, empty], axis=0)
+
+    selfs, lines = [], [[] for _ in range(links)]
+    for t in range(tiles):
+        cut = slice(LANES * t, LANES * (t + 1))
+        d_real, d_imag = adm_ref[0, 0, :, cut], adm_ref[1, 0, :, cut]
+        selfs.append(stacked(d_real, d_imag))
+        for k in range(links):
+            l_real, l_imag = adm_ref[0, 1 + k, :, cut], adm_ref[1, 1 + k, :, cut]
+            lines[k].append(stacked(d_real * l_real - d_imag * l_imag, d_real * l_imag + d_imag * l_real))
+    for m in range(-1, nh + 1):
+        line_part = jnp.zeros((2 * deep, LANES), jnp.float32)
+        for k in range(links):
+            inside = jnp.logical_and(lane >= inner * k, lane < inner * (k + 1))
+            line_part = jnp.where(inside, window(lines[k], sub * m - REACH, inner * k), line_part)
+        self_part = jnp.where(lane < outer, window(selfs, sub * m - 2 * REACH, 0), 0.0)
+        parcels[m + 1] = jnp.concatenate([line_part, self_part], axis=0).astype(jnp.bfloat16)
+
     pl.semaphore_wait(barrier, nh - 1 + nh * has_left.astype(jnp.int32) + nh * has_right.astype(jnp.int32))
 
     def remote(src, dst, out, into, d, by):
@@ -181,9 +237,17 @@
     def spec_copy(d, slot, by, out, into):
         return remote(send.at[d], recv.at[slot], out, into, d, by)
 
-    def ret_copy(d, source):
-        place = next_ref.at[:, pl.ds(source * hl, hl)]
-        return remote(send_back.at[d], place, 6, 6, d, y)
+    def parcel_copy(d):
+        return remote(parcels.at[d + 1], parcel_recv.at[me], 6, 6, d, y)
+
+    def edge_copy(side, d, by):
+        own_parcel = parcels.at[nh + 1 if side == 0 else 0]
+        return remote(own_parcel, parcel_edge.at[me], 11 + side, 11, d, by)
+
+    def near_copy(side, d, by):
+        return remote(send, near_spec.at[side], 13 + side, 13 + side, d, by)
+
+    up, down = lax.rem(y + 1, ny), lax.rem(y + ny - 1, ny)
 
     def side_copies(side):
         by = y + 1 if side == 0 else y - 1
@@ -204,7 +268,33 @@
             copy.start()
 
     each(1, lambda s: bus_copy(peer(s), me + 1, y, 0, 0).start())
+    each(1, lambda s: parcel_copy(peer(s)).start())
+
+    @pl.when(has_right)
+    def _():
+        edge_copy(0, lax.rem(me + nh - me, nh), up).start()
+
+    @pl.when(has_left)
+    def _():
+        edge_copy(1, lax.rem(me + 2 * nh - 1 - me, nh), down).start()
+
     each(1, lambda s: spec_copy(peer(s), me + 1, y, 3, 3).start())
+
+    @pl.when(me < nh - 1)
+    def _():
+        near_copy(0, peer(1), y).start()
+
+    @pl.when(me > 0)
+    def _():
+        near_copy(1, peer(nh - 1), y).start()
+
+    @pl.when(send_right)
+    def _():
+        near_copy(0, peer(1), up).start()
+
+    @pl.when(send_left)
+    def _():
+        near_copy(1, peer(nh - 1), down).start()
 
     @pl.when(send_right)
     def _():
@@ -218,8 +308,8 @@
 
     recv[me + 1] = send[me]
     buses[me + 1] = my_bus[...]
-
-    lane = lax.broadcasted_iota(jnp.int32, (1, LANES), 1)
+    parcel_recv[me] = parcels[me + 1]
+
     is_right = lane < LANES // 2
 
     def adm_row(p, k, h, t, beyond):
@@ -321,15 +411,103 @@
     row = lax.broadcasted_iota(jnp.int32, (rows, LANES), 0)
     is_real = row % 8 < conv
     base = jnp.bitwise_and((row // 8 - 1) * sub, 2 * LANES - 1)
-    own = 8 * around
-    spread, gather = [], []
+    spread = []
     for t in range(tiles):
         near = buses[around * t : around * (t + 1) + 2].astype(jnp.float32).reshape(rows, LANES)
         at_bus = base + near.astype(jnp.int32)
         hits = [jnp.where(at_bus == lane + shift, 1.0, 0.0) for shift in (0, LANES)]
         spread.append(jnp.concatenate([hit.T for hit in hits], axis=0).astype(jnp.bfloat16))
-        picks = [jnp.where(is_real, hits[0], 0.0), jnp.where(is_real, 0.0, hits[0])]
-        gather.append(jnp.concatenate(picks, axis=1)[8 : 8 + own].astype(jnp.bfloat16))
+
+    off_tiles = [off_side[0].astype(jnp.float32)]
+    off_tiles += [off_ref[:, LANES * t : LANES * (t + 1)].astype(jnp.float32) for t in range(tiles)]
+    off_tiles.append(off_side[1].astype(jnp.float32))
+    for m in range(nh):
+        offsets = jnp.zeros((1, LANES), jnp.float32)
+        for k in range(links):
+            inside = jnp.logical_and(lane >= inner * k, lane < inner * (k + 1))
+            offsets = jnp.where(inside, window(off_tiles, LANES + sub * m - REACH, inner * k)[k : k + 1], offsets)
+        off_row8[m] = jnp.broadcast_to(offsets, (8, LANES))
+    used = lane < inner * links
+    in_inner = lax.rem(lane, inner)
+    ends = in_inner + off_row8[me][0:1].astype(jnp.int32)
+    tall = lax.broadcasted_iota(jnp.int32, (LANES, LANES), 0)
+    to_inner = jnp.logical_and(jnp.logical_and(lax.rem(tall, inner) == ends, tall < inner * links), used)
+    to_outer = jnp.logical_and(tall == ends + REACH, used)
+    hops = jnp.concatenate([jnp.where(to_inner, 1.0, 0.0), jnp.where(to_outer, 1.0, 0.0)], axis=0)
+    hops = hops.astype(jnp.bfloat16)
+    group = 2 * conv * hl
+    near_rows = []
+    for j in range(3):
+        near = buses[me + j].astype(jnp.float32) + float(sub * (j - 1) + 2 * REACH)
+        near_rows += [near] * hl
+    if 3 * group < LANES:
+        near_rows.append(jnp.full((LANES - 3 * group, LANES), -1.0, jnp.float32))
+    hit = jnp.concatenate(near_rows, axis=0).astype(jnp.int32) == lane
+    part_one = lax.rem(tall, 8) < conv
+    picks = [jnp.where(jnp.logical_and(hit, part_one), 1.0, 0.0)]
+    picks.append(jnp.where(jnp.logical_and(hit, jnp.logical_not(part_one)), 1.0, 0.0))
+    picks = jnp.concatenate(picks, axis=0).astype(jnp.bfloat16)
+    size = 2 * deep * conv
+    order = LANES // size
+    wanted = tall // size * size + lax.rem(tall, conv) * 2 * deep + lax.rem(tall, size) // conv
+    shuffle = jnp.where(wanted == lane, 1.0, 0.0).astype(jnp.bfloat16)
+
+    all_of(parcel_recv, nh - 1, 6, 6).wait_recv()
+
+    @pl.when(jnp.logical_or(send_left, send_right))
+    def _():
+        all_of(parcel_edge, nh, 11, 11).wait_recv()
+
+    parcel = parcel_recv[...].astype(jnp.float32) + parcel_edge[...].astype(jnp.float32)
+    line_all = parcel[:, : 2 * deep]
+    self_all = parcel[:, 2 * deep :]
+    real_row = lax.broadcasted_iota(jnp.int32, (nh, 2 * deep, LANES), 1) < deep
+
+    def swap(x):
+        return pltpu.roll(x, deep, 1)
+
+    def turned(x):
+        return jnp.where(real_row, -swap(x), swap(x))
+
+    line_turned, self_turned = turned(line_all), turned(self_all)
+
+    def times(x, y_all, y_turned):
+        other = swap(x)
+        return jnp.where(real_row, x, other) * y_all + jnp.where(real_row, other, x) * y_turned
+
+    flat, full = (nh * 2 * deep, LANES), (nh, 2 * deep, LANES)
+    numbers_own = [bus_ref[c] - first for c in range(conv)]
+    begins = []
+    for c in range(conv):
+        at_line = jnp.logical_and(in_inner == numbers_own[c] + REACH, used)
+        begins.append(jnp.where(at_line, line_all.reshape(flat), 0.0).astype(jnp.bfloat16))
+    one = lax.dot_general(jnp.concatenate(begins, axis=0), hops, across, preferred_element_type=jnp.float32)
+    nexts = []
+    for c in range(conv):
+        here = one[flat[0] * c : flat[0] * (c + 1), :LANES].reshape(full)
+        nexts.append(times(here, line_all, line_turned).reshape(flat).astype(jnp.bfloat16))
+    two = lax.dot_general(
+        jnp.concatenate(nexts, axis=0), hops[LANES:], across, preferred_element_type=jnp.float32
+    )
+    rows_at = []
+    for c in range(conv):
+        cut = slice(flat[0] * c, flat[0] * (c + 1))
+        start = jnp.where(jnp.logical_and(real_row, lane == numbers_own[c] + 2 * REACH), 1.0, 0.0)
+        reached = start + (one[cut, LANES:] + two[cut]).reshape(full)
+        rows_at.append(times(reached, self_all, self_turned).reshape(flat).astype(jnp.bfloat16))
+    taken = lax.dot_general(jnp.concatenate(rows_at, axis=0), picks, across, preferred_element_type=jnp.float32)
+    harm_row = lax.rem(lax.broadcasted_iota(jnp.int32, full, 1), deep)
+    same = harm_row == lax.rem(lane // 8, hl)
+    answer = []
+    for c in range(conv):
+        cut = slice(flat[0] * c, flat[0] * (c + 1))
+        whole = taken[cut, :LANES].reshape(full) + turned(taken[cut, LANES:].reshape(full))
+        answer.append(jnp.where(same, whole, 0.0).astype(jnp.bfloat16))
+    sorted_rows = []
+    for b in range(nh // order):
+        block_rows = [answer[c][order * b + i] for i in range(order) for c in range(conv)]
+        mixed = jnp.dot(shuffle, jnp.concatenate(block_rows, axis=0), preferred_element_type=jnp.float32)
+        sorted_rows.append(mixed.astype(jnp.bfloat16))
 
     all_of(recv, nh - 1, 3, 3).wait_recv()
 
@@ -361,16 +539,30 @@
             imag = both[:LANES, LANES:] + both[LANES:, :LANES]
             now.append(jnp.concatenate([real, imag], axis=0).astype(jnp.bfloat16))
         volts_now.append(now)
-        at_conv = jnp.dot(gather[t], jnp.concatenate(now, axis=1), preferred_element_type=jnp.float32)
-        for h in range(hl):
-            chosen = at_conv[:, LANES * h : LANES * (h + 1)].reshape(around, 2, conv, LANES)
-            send_back[around * t : around * (t + 1), :, h] = chosen.astype(jnp.bfloat16)
-    each(1, lambda s: ret_copy(peer(s), me).start())
-    next_ref[:, pl.ds(me * hl, hl)] = send_back[me]
     for t in range(tiles):
         for h in range(hl):
             out_ref[:, h, LANES * t : LANES * (t + 1)] = volts_now[t][h].reshape(2, LANES, LANES)
 
+    @pl.when(near_left)
+    def _():
+        near_copy(0, me, y).wait_recv()
+
+    @pl.when(near_right)
+    def _():
+        near_copy(1, me, y).wait_recv()
+
+    for source in range(nh):
+        around_here = jnp.concatenate(
+            [near_spec[0, source].reshape(group, LANES), send[source].reshape(group, LANES)]
+            + [near_spec[1, source].reshape(group, LANES)],
+            axis=0,
+        )
+        at = size * (source % order)
+        mine = sorted_rows[source // order][at : at + size, : 3 * group]
+        at_conv = jnp.dot(mine, around_here, preferred_element_type=jnp.float32)
+        at_conv = at_conv.reshape(2, deep, conv, LANES).astype(jnp.bfloat16)
+        next_ref[:, hl * source : hl * (source + 1)] = at_conv[:, :hl]
+
     all_of(buses, nh - 1, 0, 0).wait_send()
     all_of(recv, nh - 1, 3, 3).wait_send()
 
@@ -394,8 +586,23 @@
         all_of(buses, nh, 2, 2).wait_send()
         all_of(recv, nh, 5, 5).wait_send()
 
-    all_of(send_back, nh - 1, 6, 6).wait_send()
-    all_of(send_back, nh - 1, 6, 6).wait_recv()
+    all_of(parcel_recv, nh - 1, 6, 6).wait_send()
+
+    @pl.when(has_right)
+    def _():
+        edge_copy(0, me, y).wait_send()
+
+    @pl.when(has_left)
+    def _():
+        edge_copy(1, me, y).wait_send()
+
+    @pl.when(near_right)
+    def _():
+        near_copy(0, me, y).wait_send()
+
+    @pl.when(near_left)
+    def _():
+        near_copy(1, me, y).wait_send()
 
 
 def store(volt_ref, next_ref, volt_out, next_out, sems):
@@ -413,6 +620,7 @@
     block = admittance.shape[3]
     tiles = block // LANES
     around = LANES * nh // block
+    deep = max(hl, 4)
     span = 2 * orders
     basis = make_basis(orders)
     regrouped = basis.reshape(2, orders, NT).transpose(1, 0, 2).reshape(span, NT)
@@ -446,10 +654,14 @@
             pltpu.VMEM((2, link_offset.shape[0], LANES), jnp.int32),
             pltpu.VMEM((hl, tiles, 2 * LANES, 4 * LANES), bf16),
             pltpu.VMEM((hl, tiles, 2 * LANES, 2 * LANES), bf16),
-            pltpu.VMEM((nh, 2, hl, conv, LANES), bf16),
+            pltpu.VMEM((nh + 2, 4 * deep, LANES), bf16),
+            pltpu.VMEM((nh, 4 * deep, LANES), bf16),
+            pltpu.VMEM((nh, 4 * deep, LANES), bf16),
+            pltpu.VMEM((2, nh, hl, 8, LANES), bf16),
+            pltpu.VMEM((nh, 8, LANES), jnp.float32),
             dma((9,)),
-            dma((11,)),
-            dma((11,)),
+            dma((15,)),
+            dma((15,)),
         ],
         compiler_params=pltpu.CompilerParams(collective_id=0, has_side_effects=True, vmem_limit_bytes=56 * 2**20),
         name="power_flow",

time: 21.4 us -> 18.2 us (0.85)
  Pallas kernels: 20.6 us -> 17.4 us
    pallas_call x1, Pallas kernels: 19.8 us -> 16.6 us  [local(): pl.pallas_call(functools.partial(kernel, nh, ny), out_shape=(pltpu.VMEM(v...]
where the time goes in v4:
time: 18.2 us; the launch traced here: 18 us
  Pallas kernels  17.4 us (96%)
  between operations  0.64 us (4%)
    pallas_call x1, Pallas kernels, local(): pl.pallas_call(functools.partial(kernel, nh, ny), out_shape=(pltpu.VMEM(v...  16.6 us
    pallas_call x1, Pallas kernels, local(): pl.pallas_call(store, out_shape=(jax.ShapeDtypeStruct(volt_shape, bf16),...  0.86 us

profile of v4, /device:TPU:0, one launch (start us, length us, event | category | flops | bytes accessed | tf_op | source)
XLA Modules:
  0.0 18.0 jit_solution(876018077768638395)
XLA Ops:
  0.6 16.6 %power_flow.1 = (bf16[2,4,256,128]{3,2,1,0:T(8,128)(2,1)S(1)}, bf16[2,64,4,128]{3,2,1,0:T(4,128)(2,1)S(1)}) custom-call(bf16[512,128]{1,0:T(8,128)(2,1)} %bitcast.1, f32[4,128]{1,0:T(4,128)} %power_hbm.1, s32[4]{0:T(128)} %type_hbm.1, f32[8]{0:T(128)} %steep_hbm.1, s32[4]{0:T(128)} %bus_hbm.1, f32[2,4,4,256]{3,2,1,0:T(4,128)} %adm_hbm.1, s32[3,256]{1,0:T(4,128)} %off_hbm.1, ...), custom_call_target="tpu_custom_call" | custom-call | tf_op jit(solution)/shard_map/power_flow/pallas_call | solution.py:632
  17.2 0.9 %store_results.1 = (bf16[2,4,256,128]{3,2,1,0:T(8,128)(2,1)}, bf16[2,64,4,128]{3,2,1,0:T(4,128)(2,1)}) custom-call(bf16[2,4,256,128]{3,2,1,0:T(8,128)(2,1)S(1)} %get-tuple-element.4.volt_ref, bf16[2,64,4,128]{3,2,1,0:T(4,128)(2,1)S(1)} %get-tuple-element.5.next_ref), custom_call_target="tpu_custom_call" | custom-call | tf_op jit(solution)/shard_map/store_results/pallas_call | solution.py:679

commit v5 on v4

--- a/solution.py
+++ b/solution.py
@@ -73,7 +73,7 @@
     tiles = block // LANES
     around = LANES // sub
     rows = 8 * (around + 2)
-    deep = parcels.shape[1] // 4
+    deep = parcels.shape[1] // 3
     inner, outer = sub + 2 * REACH, sub + 4 * REACH
     has_left = y > 0
     has_right = y < ny - 1
@@ -148,12 +148,14 @@
     def _():
         near_spec[1] = jnp.zeros(near_spec.shape[1:], near_spec.dtype)
 
-    for load in loads[:6]:
-        load.wait()
+    loads[0].wait()
     span = volt_ref.shape[0] // conv
     wide[0 : span * conv] = volt_ref[...].astype(jnp.float32)
     for c in range(conv):
         volts[:, LANES * c : LANES * (c + 1)] = wide[pl.ds(c, span, stride=conv), :].astype(jnp.bfloat16)
+
+    for load in loads[1:5]:
+        load.wait()
 
     def steepness(c):
         value = steep_ref[0]
@@ -163,6 +165,7 @@
 
     steep = jnp.concatenate([steepness(c) for c in range(conv)], axis=1)
     power = jnp.concatenate([power_ref[c : c + 1, :] for c in range(conv)], axis=1) * NT ** (-0.5)
+    loads[5].wait()
     part = NT // CHUNKS
     spectra = jnp.zeros((span, conv * LANES), jnp.float32)
     for q in range(CHUNKS):
@@ -204,20 +207,24 @@
         empty = jnp.zeros((deep - hl, LANES), jnp.float32)
         return jnp.concatenate([real, empty, imag, empty], axis=0)
 
-    selfs, lines = [], [[] for _ in range(links)]
+    selfs, lines = [[], []], [[] for _ in range(links)]
     for t in range(tiles):
         cut = slice(LANES * t, LANES * (t + 1))
         d_real, d_imag = adm_ref[0, 0, :, cut], adm_ref[1, 0, :, cut]
-        selfs.append(stacked(d_real, d_imag))
+        for p, value in enumerate((d_real, d_imag)):
+            if deep > hl:
+                value = jnp.concatenate([value, jnp.zeros((deep - hl, LANES), jnp.float32)], axis=0)
+            selfs[p].append(value)
         for k in range(links):
             l_real, l_imag = adm_ref[0, 1 + k, :, cut], adm_ref[1, 1 + k, :, cut]
             lines[k].append(stacked(d_real * l_real - d_imag * l_imag, d_real * l_imag + d_imag * l_real))
     for m in range(-1, nh + 1):
-        line_part = jnp.zeros((2 * deep, LANES), jnp.float32)
+        line_part = numbers if 2 * deep == 8 else jnp.concatenate([numbers] * (deep // 4), axis=0)
         for k in range(links):
             inside = jnp.logical_and(lane >= inner * k, lane < inner * (k + 1))
             line_part = jnp.where(inside, window(lines[k], sub * m - REACH, inner * k), line_part)
-        self_part = jnp.where(lane < outer, window(selfs, sub * m - 2 * REACH, 0), 0.0)
+        self_parts = [window(selfs[p], sub * m - 2 * REACH, outer * p) for p in range(2)]
+        self_part = jnp.where(lane < outer, self_parts[0], jnp.where(lane < 2 * outer, self_parts[1], 0.0))
         parcels[m + 1] = jnp.concatenate([line_part, self_part], axis=0).astype(jnp.bfloat16)
 
     pl.semaphore_wait(barrier, nh - 1 + nh * has_left.astype(jnp.int32) + nh * has_right.astype(jnp.int32))
@@ -267,35 +274,6 @@
         for copy in side_copies(1):
             copy.start()
 
-    each(1, lambda s: bus_copy(peer(s), me + 1, y, 0, 0).start())
-    each(1, lambda s: parcel_copy(peer(s)).start())
-
-    @pl.when(has_right)
-    def _():
-        edge_copy(0, lax.rem(me + nh - me, nh), up).start()
-
-    @pl.when(has_left)
-    def _():
-        edge_copy(1, lax.rem(me + 2 * nh - 1 - me, nh), down).start()
-
-    each(1, lambda s: spec_copy(peer(s), me + 1, y, 3, 3).start())
-
-    @pl.when(me < nh - 1)
-    def _():
-        near_copy(0, peer(1), y).start()
-
-    @pl.when(me > 0)
-    def _():
-        near_copy(1, peer(nh - 1), y).start()
-
-    @pl.when(send_right)
-    def _():
-        near_copy(0, peer(1), up).start()
-
-    @pl.when(send_left)
-    def _():
-        near_copy(1, peer(nh - 1), down).start()
-
     @pl.when(send_right)
     def _():
         each(0, lambda d: bus_copy(d, 0, y + 1, 1, 1).start())
@@ -306,8 +284,21 @@
         each(0, lambda d: bus_copy(d, nh + 1, y - 1, 2, 2).start())
         each(0, lambda d: spec_copy(d, nh + 1, y - 1, 5, 5).start())
 
+    for s in range(1, nh):
+        parcel_copy(peer(s)).start()
+
+    @pl.when(has_right)
+    def _():
+        edge_copy(0, lax.rem(me + nh - me, nh), up).start()
+
+    @pl.when(has_left)
+    def _():
+        edge_copy(1, lax.rem(me + 2 * nh - 1 - me, nh), down).start()
+
+    for s in range(1, nh):
+        spec_copy(peer(s), me + 1, y, 3, 3).start()
+
     recv[me + 1] = send[me]
-    buses[me + 1] = my_bus[...]
     parcel_recv[me] = parcels[me + 1]
 
     is_right = lane < LANES // 2
@@ -356,6 +347,22 @@
             weights[h, t, LANES + 16 : 2 * LANES - 16, :] = jnp.zeros((LANES - 32, 4 * LANES), jnp.bfloat16)
             for at in (LANES, 3 * LANES):
                 weights[h, t, 16 : LANES - 16, at : at + LANES] = jnp.zeros((LANES - 32, LANES), jnp.bfloat16)
+
+    @pl.when(me < nh - 1)
+    def _():
+        near_copy(0, peer(1), y).start()
+
+    @pl.when(me > 0)
+    def _():
+        near_copy(1, peer(nh - 1), y).start()
+
+    @pl.when(send_right)
+    def _():
+        near_copy(0, peer(1), up).start()
+
+    @pl.when(send_left)
+    def _():
+        near_copy(1, peer(nh - 1), down).start()
 
     @pl.when(has_left)
     def _():
@@ -398,25 +405,9 @@
             resp[h, t, 0:LANES] = (real * d_real - imag * d_imag).astype(jnp.bfloat16)
             resp[h, t, LANES:] = (real * d_imag + imag * d_real).astype(jnp.bfloat16)
 
-    all_of(buses, nh - 1, 0, 0).wait_recv()
-
-    @pl.when(has_left)
-    def _():
-        bus_copy(0, 0, y, 1, 1).wait_recv()
-
-    @pl.when(has_right)
-    def _():
-        bus_copy(0, nh + 1, y, 2, 2).wait_recv()
-
-    row = lax.broadcasted_iota(jnp.int32, (rows, LANES), 0)
-    is_real = row % 8 < conv
-    base = jnp.bitwise_and((row // 8 - 1) * sub, 2 * LANES - 1)
-    spread = []
-    for t in range(tiles):
-        near = buses[around * t : around * (t + 1) + 2].astype(jnp.float32).reshape(rows, LANES)
-        at_bus = base + near.astype(jnp.int32)
-        hits = [jnp.where(at_bus == lane + shift, 1.0, 0.0) for shift in (0, LANES)]
-        spread.append(jnp.concatenate([hit.T for hit in hits], axis=0).astype(jnp.bfloat16))
+    all_of(parcel_recv, nh - 1, 6, 6).wait_recv()
+    given = parcel_recv[...].astype(jnp.float32)
+    buses[1 : nh + 1] = jnp.broadcast_to(given[:, :8, LANES - 1 :], (nh, 8, LANES)).astype(jnp.bfloat16)
 
     off_tiles = [off_side[0].astype(jnp.float32)]
     off_tiles += [off_ref[:, LANES * t : LANES * (t + 1)].astype(jnp.float32) for t in range(tiles)]
@@ -435,32 +426,19 @@
     to_outer = jnp.logical_and(tall == ends + REACH, used)
     hops = jnp.concatenate([jnp.where(to_inner, 1.0, 0.0), jnp.where(to_outer, 1.0, 0.0)], axis=0)
     hops = hops.astype(jnp.bfloat16)
-    group = 2 * conv * hl
-    near_rows = []
-    for j in range(3):
-        near = buses[me + j].astype(jnp.float32) + float(sub * (j - 1) + 2 * REACH)
-        near_rows += [near] * hl
-    if 3 * group < LANES:
-        near_rows.append(jnp.full((LANES - 3 * group, LANES), -1.0, jnp.float32))
-    hit = jnp.concatenate(near_rows, axis=0).astype(jnp.int32) == lane
-    part_one = lax.rem(tall, 8) < conv
-    picks = [jnp.where(jnp.logical_and(hit, part_one), 1.0, 0.0)]
-    picks.append(jnp.where(jnp.logical_and(hit, jnp.logical_not(part_one)), 1.0, 0.0))
-    picks = jnp.concatenate(picks, axis=0).astype(jnp.bfloat16)
     size = 2 * deep * conv
     order = LANES // size
     wanted = tall // size * size + lax.rem(tall, conv) * 2 * deep + lax.rem(tall, size) // conv
     shuffle = jnp.where(wanted == lane, 1.0, 0.0).astype(jnp.bfloat16)
 
-    all_of(parcel_recv, nh - 1, 6, 6).wait_recv()
-
     @pl.when(jnp.logical_or(send_left, send_right))
     def _():
         all_of(parcel_edge, nh, 11, 11).wait_recv()
 
-    parcel = parcel_recv[...].astype(jnp.float32) + parcel_edge[...].astype(jnp.float32)
+    parcel = given + parcel_edge[...].astype(jnp.float32)
     line_all = parcel[:, : 2 * deep]
-    self_all = parcel[:, 2 * deep :]
+    self_both = parcel[:, 2 * deep :]
+    self_all = jnp.concatenate([self_both, pltpu.roll(self_both, LANES - outer, 2)], axis=1)
     real_row = lax.broadcasted_iota(jnp.int32, (nh, 2 * deep, LANES), 1) < deep
 
     def swap(x):
@@ -495,6 +473,26 @@
         start = jnp.where(jnp.logical_and(real_row, lane == numbers_own[c] + 2 * REACH), 1.0, 0.0)
         reached = start + (one[cut, LANES:] + two[cut]).reshape(full)
         rows_at.append(times(reached, self_all, self_turned).reshape(flat).astype(jnp.bfloat16))
+    @pl.when(has_left)
+    def _():
+        bus_copy(0, 0, y, 1, 1).wait_recv()
+
+    @pl.when(has_right)
+    def _():
+        bus_copy(0, nh + 1, y, 2, 2).wait_recv()
+
+    group = 2 * conv * hl
+    near_rows = []
+    for j in range(3):
+        near = buses[me + j].astype(jnp.float32) + float(sub * (j - 1) + 2 * REACH)
+        near_rows += [near] * hl
+    if 3 * group < LANES:
+        near_rows.append(jnp.full((LANES - 3 * group, LANES), -1.0, jnp.float32))
+    hit = jnp.concatenate(near_rows, axis=0).astype(jnp.int32) == lane
+    part_one = lax.rem(tall, 8) < conv
+    picks = [jnp.where(jnp.logical_and(hit, part_one), 1.0, 0.0)]
+    picks.append(jnp.where(jnp.logical_and(hit, jnp.logical_not(part_one)), 1.0, 0.0))
+    picks = jnp.concatenate(picks, axis=0).astype(jnp.bfloat16)
     taken = lax.dot_general(jnp.concatenate(rows_at, axis=0), picks, across, preferred_element_type=jnp.float32)
     harm_row = lax.rem(lax.broadcasted_iota(jnp.int32, full, 1), deep)
     same = harm_row == lax.rem(lane // 8, hl)
@@ -509,6 +507,17 @@
         mixed = jnp.dot(shuffle, jnp.concatenate(block_rows, axis=0), preferred_element_type=jnp.float32)
         sorted_rows.append(mixed.astype(jnp.bfloat16))
 
+    row = lax.broadcasted_iota(jnp.int32, (rows, LANES), 0)
+    is_real = row % 8 < conv
+    base = jnp.bitwise_and((row // 8 - 1) * sub, 2 * LANES - 1)
+    spread = []
+    for t in range(tiles):
+        near = buses[around * t : around * (t + 1) + 2].astype(jnp.float32).reshape(rows, LANES)
+        at_bus = base + near.astype(jnp.int32)
+        hits = [jnp.where(at_bus == lane + shift, 1.0, 0.0) for shift in (0, LANES)]
+        spread.append(jnp.concatenate([hit.T for hit in hits], axis=0).astype(jnp.bfloat16))
+
+
     all_of(recv, nh - 1, 3, 3).wait_recv()
 
     @pl.when(has_left)
@@ -563,7 +572,6 @@
         at_conv = at_conv.reshape(2, deep, conv, LANES).astype(jnp.bfloat16)
         next_ref[:, hl * source : hl * (source + 1)] = at_conv[:, :hl]
 
-    all_of(buses, nh - 1, 0, 0).wait_send()
     all_of(recv, nh - 1, 3, 3).wait_send()
 
     @pl.when(has_right)
@@ -654,9 +662,9 @@
             pltpu.VMEM((2, link_offset.shape[0], LANES), jnp.int32),
             pltpu.VMEM((hl, tiles, 2 * LANES, 4 * LANES), bf16),
             pltpu.VMEM((hl, tiles, 2 * LANES, 2 * LANES), bf16),
-            pltpu.VMEM((nh + 2, 4 * deep, LANES), bf16),
-            pltpu.VMEM((nh, 4 * deep, LANES), bf16),
-            pltpu.VMEM((nh, 4 * deep, LANES), bf16),
+            pltpu.VMEM((nh + 2, 3 * deep, LANES), bf16),
+            pltpu.VMEM((nh, 3 * deep, LANES), bf16),
+            pltpu.VMEM((nh, 3 * deep, LANES), bf16),
             pltpu.VMEM((2, nh, hl, 8, LANES), bf16),
             pltpu.VMEM((nh, 8, LANES), jnp.float32),
             dma((9,)),

time: 18.2 us -> 15.9 us (0.87)
  Pallas kernels: 17.4 us -> 15.1 us
    pallas_call x1, Pallas kernels: 16.6 us -> 14.2 us  [local(): pl.pallas_call(functools.partial(kernel, nh, ny), out_shape=(pltpu.VMEM(v...]
where the time goes in v5:
time: 15.9 us; the launch traced here: 15.7 us
  Pallas kernels  15.1 us (95%)
  between operations  0.64 us (4%)
    pallas_call x1, Pallas kernels, local(): pl.pallas_call(functools.partial(kernel, nh, ny), out_shape=(pltpu.VMEM(v...  14.2 us
    pallas_call x1, Pallas kernels, local(): pl.pallas_call(store, out_shape=(jax.ShapeDtypeStruct(volt_shape, bf16),...  0.86 us

profile of v5, /device:TPU:0, one launch (start us, length us, event | category | flops | bytes accessed | tf_op | source)
XLA Modules:
  0.0 15.7 jit_solution(1813246654781797177)
XLA Ops:
  0.6 14.2 %power_flow.1 = (bf16[2,4,256,128]{3,2,1,0:T(8,128)(2,1)S(1)}, bf16[2,64,4,128]{3,2,1,0:T(4,128)(2,1)S(1)}) custom-call(bf16[512,128]{1,0:T(8,128)(2,1)} %bitcast.1, f32[4,128]{1,0:T(4,128)} %power_hbm.1, s32[4]{0:T(128)} %type_hbm.1, f32[8]{0:T(128)} %steep_hbm.1, s32[4]{0:T(128)} %bus_hbm.1, f32[2,4,4,256]{3,2,1,0:T(4,128)} %adm_hbm.1, s32[3,256]{1,0:T(4,128)} %off_hbm.1, ...), custom_call_target="tpu_custom_call" | custom-call | tf_op jit(solution)/shard_map/power_flow/pallas_call | solution.py:640
  14.9 0.9 %store_results.1 = (bf16[2,4,256,128]{3,2,1,0:T(8,128)(2,1)}, bf16[2,64,4,128]{3,2,1,0:T(4,128)(2,1)}) custom-call(bf16[2,4,256,128]{3,2,1,0:T(8,128)(2,1)S(1)} %get-tuple-element.4.volt_ref, bf16[2,64,4,128]{3,2,1,0:T(4,128)(2,1)S(1)} %get-tuple-element.5.next_ref), custom_call_target="tpu_custom_call" | custom-call | tf_op jit(solution)/shard_map/store_results/pallas_call | solution.py:687

commit v6 on v5

--- a/solution.py
+++ b/solution.py
@@ -83,15 +83,15 @@
     send_left = jnp.logical_and(has_left, me == 0)
 
     pairs = (
+        (bus_hbm, bus_ref),
+        (adm_hbm, adm_ref),
+        (off_hbm, off_ref),
         (volt_hbm, volt_ref),
         (fwd_hbm, fwd_ref),
         (type_hbm, type_ref),
         (steep_hbm, steep_ref),
         (power_hbm, power_ref),
         (inv_hbm, inv_ref),
-        (bus_hbm, bus_ref),
-        (adm_hbm, adm_ref),
-        (off_hbm, off_ref),
     )
     loads = [pltpu.make_async_copy(src, dst, load_sem.at[i]) for i, (src, dst) in enumerate(pairs)]
     for load in loads:
@@ -148,38 +148,7 @@
     def _():
         near_spec[1] = jnp.zeros(near_spec.shape[1:], near_spec.dtype)
 
-    loads[0].wait()
-    span = volt_ref.shape[0] // conv
-    wide[0 : span * conv] = volt_ref[...].astype(jnp.float32)
-    for c in range(conv):
-        volts[:, LANES * c : LANES * (c + 1)] = wide[pl.ds(c, span, stride=conv), :].astype(jnp.bfloat16)
-
-    for load in loads[1:5]:
-        load.wait()
-
-    def steepness(c):
-        value = steep_ref[0]
-        for kind in range(1, steep_ref.shape[0]):
-            value = jnp.where(type_ref[c] == kind, steep_ref[kind], value)
-        return jnp.full((1, LANES), value, jnp.float32)
-
-    steep = jnp.concatenate([steepness(c) for c in range(conv)], axis=1)
-    power = jnp.concatenate([power_ref[c : c + 1, :] for c in range(conv)], axis=1) * NT ** (-0.5)
-    loads[5].wait()
-    part = NT // CHUNKS
-    spectra = jnp.zeros((span, conv * LANES), jnp.float32)
-    for q in range(CHUNKS):
-        wave = jnp.dot(fwd_ref[part * q : part * (q + 1), :], volts[...], preferred_element_type=jnp.float32)
-        now = jnp.tanh(steep * wave).astype(jnp.bfloat16)
-        spectra = spectra + jnp.dot(
-            inv_ref[:, part * q : part * (q + 1)], now, preferred_element_type=jnp.float32
-        )
-    spectra = spectra * power
-    for c in range(conv):
-        wide[pl.ds(c, span, stride=conv), :] = spectra[:, LANES * c : LANES * (c + 1)]
-    send[...] = wide[0 : span * conv].reshape(nh, hl, 8, LANES).astype(jnp.bfloat16)
-
-    for load in loads[6:]:
+    for load in loads[:3]:
         load.wait()
     first = (y * nh + me) * sub
     row8 = lax.broadcasted_iota(jnp.int32, (8, LANES), 0) % conv
@@ -226,6 +195,37 @@
         self_parts = [window(selfs[p], sub * m - 2 * REACH, outer * p) for p in range(2)]
         self_part = jnp.where(lane < outer, self_parts[0], jnp.where(lane < 2 * outer, self_parts[1], 0.0))
         parcels[m + 1] = jnp.concatenate([line_part, self_part], axis=0).astype(jnp.bfloat16)
+
+    loads[3].wait()
+    span = volt_ref.shape[0] // conv
+    wide[0 : span * conv] = volt_ref[...].astype(jnp.float32)
+    for c in range(conv):
+        volts[:, LANES * c : LANES * (c + 1)] = wide[pl.ds(c, span, stride=conv), :].astype(jnp.bfloat16)
+
+    for load in loads[4:8]:
+        load.wait()
+
+    def steepness(c):
+        value = steep_ref[0]
+        for kind in range(1, steep_ref.shape[0]):
+            value = jnp.where(type_ref[c] == kind, steep_ref[kind], value)
+        return jnp.full((1, LANES), value, jnp.float32)
+
+    steep = jnp.concatenate([steepness(c) for c in range(conv)], axis=1)
+    power = jnp.concatenate([power_ref[c : c + 1, :] for c in range(conv)], axis=1) * NT ** (-0.5)
+    loads[8].wait()
+    part = NT // CHUNKS
+    spectra = jnp.zeros((span, conv * LANES), jnp.float32)
+    for q in range(CHUNKS):
+        wave = jnp.dot(fwd_ref[part * q : part * (q + 1), :], volts[...], preferred_element_type=jnp.float32)
+        now = jnp.tanh(steep * wave).astype(jnp.bfloat16)
+        spectra = spectra + jnp.dot(
+            inv_ref[:, part * q : part * (q + 1)], now, preferred_element_type=jnp.float32
+        )
+    spectra = spectra * power
+    for c in range(conv):
+        wide[pl.ds(c, span, stride=conv), :] = spectra[:, LANES * c : LANES * (c + 1)]
+    send[...] = wide[0 : span * conv].reshape(nh, hl, 8, LANES).astype(jnp.bfloat16)
 
     pl.semaphore_wait(barrier, nh - 1 + nh * has_left.astype(jnp.int32) + nh * has_right.astype(jnp.int32))
 

time: 15.9 us -> 15.9 us (level)
  the two profiles are of different devices: /device:TPU:0 before, /device:TPU:9 now
where the time goes in v6:
time: 15.9 us; the launch traced here: 15.8 us
  Pallas kernels  15.1 us (95%)
  between operations  0.64 us (4%)
    pallas_call x1, Pallas kernels, local(): pl.pallas_call(functools.partial(kernel, nh, ny), out_shape=(pltpu.VMEM(v...  14.3 us
    pallas_call x1, Pallas kernels, local(): pl.pallas_call(store, out_shape=(jax.ShapeDtypeStruct(volt_shape, bf16),...  0.86 us

profile of v6, /device:TPU:9, one launch (start us, length us, event | category | flops | bytes accessed | tf_op | source)
XLA Modules:
  0.0 15.8 jit_solution(11526473000170241480)
XLA Ops:
  0.6 14.3 %power_flow.1 = (bf16[2,4,256,128]{3,2,1,0:T(8,128)(2,1)S(1)}, bf16[2,64,4,128]{3,2,1,0:T(4,128)(2,1)S(1)}) custom-call(bf16[512,128]{1,0:T(8,128)(2,1)} %bitcast.1, f32[4,128]{1,0:T(4,128)} %power_hbm.1, s32[4]{0:T(128)} %type_hbm.1, f32[8]{0:T(128)} %steep_hbm.1, s32[4]{0:T(128)} %bus_hbm.1, f32[2,4,4,256]{3,2,1,0:T(4,128)} %adm_hbm.1, s32[3,256]{1,0:T(4,128)} %off_hbm.1, ...), custom_call_target="tpu_custom_call" | custom-call | tf_op jit(solution)/shard_map/power_flow/pallas_call | solution.py:640
  14.9 0.9 %store_results.1 = (bf16[2,4,256,128]{3,2,1,0:T(8,128)(2,1)}, bf16[2,64,4,128]{3,2,1,0:T(4,128)(2,1)}) custom-call(bf16[2,4,256,128]{3,2,1,0:T(8,128)(2,1)S(1)} %get-tuple-element.4.volt_ref, bf16[2,64,4,128]{3,2,1,0:T(4,128)(2,1)S(1)} %get-tuple-element.5.next_ref), custom_call_target="tpu_custom_call" | custom-call | tf_op jit(solution)/shard_map/store_results/pallas_call | solution.py:687

commit v7 on v6

--- a/solution.py
+++ b/solution.py
@@ -540,6 +540,14 @@
         for h in range(hl):
             mine = injected[t][:, 2 * LANES * h : 2 * LANES * (h + 1)]
             solved.append(jnp.dot(resp[h, t], mine, preferred_element_type=jnp.float32))
+    @pl.when(near_left)
+    def _():
+        near_copy(0, me, y).wait_recv()
+
+    @pl.when(near_right)
+    def _():
+        near_copy(1, me, y).wait_recv()
+
     for t in range(tiles):
         now = []
         for h in range(hl):
@@ -551,14 +559,6 @@
     for t in range(tiles):
         for h in range(hl):
             out_ref[:, h, LANES * t : LANES * (t + 1)] = volts_now[t][h].reshape(2, LANES, LANES)
-
-    @pl.when(near_left)
-    def _():
-        near_copy(0, me, y).wait_recv()
-
-    @pl.when(near_right)
-    def _():
-        near_copy(1, me, y).wait_recv()
 
     for source in range(nh):
         around_here = jnp.concatenate(

time: 15.9 us -> 16.1 us (1.013)
  the two profiles are of different devices: /device:TPU:9 before, /device:TPU:0 now
where the time goes in v7:
time: 16.1 us; the launch traced here: 15.7 us
  Pallas kernels  15.1 us (94%)
  between operations  0.64 us (4%)
    pallas_call x1, Pallas kernels, local(): pl.pallas_call(functools.partial(kernel, nh, ny), out_shape=(pltpu.VMEM(v...  14.2 us
    pallas_call x1, Pallas kernels, local(): pl.pallas_call(store, out_shape=(jax.ShapeDtypeStruct(volt_shape, bf16),...  0.86 us

profile of v7, /device:TPU:0, one launch (start us, length us, event | category | flops | bytes accessed | tf_op | source)
XLA Modules:
  0.0 15.7 jit_solution(13146809078841225666)
XLA Ops:
  0.6 14.2 %power_flow.1 = (bf16[2,4,256,128]{3,2,1,0:T(8,128)(2,1)S(1)}, bf16[2,64,4,128]{3,2,1,0:T(4,128)(2,1)S(1)}) custom-call(bf16[512,128]{1,0:T(8,128)(2,1)} %bitcast.1, f32[4,128]{1,0:T(4,128)} %power_hbm.1, s32[4]{0:T(128)} %type_hbm.1, f32[8]{0:T(128)} %steep_hbm.1, s32[4]{0:T(128)} %bus_hbm.1, f32[2,4,4,256]{3,2,1,0:T(4,128)} %adm_hbm.1, s32[3,256]{1,0:T(4,128)} %off_hbm.1, ...), custom_call_target="tpu_custom_call" | custom-call | tf_op jit(solution)/shard_map/power_flow/pallas_call | solution.py:640
  14.9 0.9 %store_results.1 = (bf16[2,4,256,128]{3,2,1,0:T(8,128)(2,1)}, bf16[2,64,4,128]{3,2,1,0:T(4,128)(2,1)}) custom-call(bf16[2,4,256,128]{3,2,1,0:T(8,128)(2,1)S(1)} %get-tuple-element.4.volt_ref, bf16[2,64,4,128]{3,2,1,0:T(4,128)(2,1)S(1)} %get-tuple-element.5.next_ref), custom_call_target="tpu_custom_call" | custom-call | tf_op jit(solution)/shard_map/store_results/pallas_call | solution.py:687
